TPU v7x, 32 devices: a whole 2x2x4 slice. The times are simulated.
32 devices in a mesh: tensor: 2 (over core), outer: 4 (over z), inter: 4 (over y, x).
Axes of the slice: x: 2, y: 2, z: 4, core: 2. Of those that a mesh axis runs over, the one named last changes fastest.
Arguments:
- features: bfloat16 [4096, 5120], P(('outer', 'inter')), may hold values from -6 to 6
- attn_weights: bfloat16 [16, 20, 256, 256], P(('outer', 'inter'), 'tensor'), may hold values from 0 to 0.0078125
- out_grad: bfloat16 [4096, 2560], P(('outer', 'inter'), 'tensor'), may hold values from -192 to 192
- storm_index: int32 [16, 96], P(('outer', 'inter')), may hold values from 0 to 255, as said below
- w_value: bfloat16 [5120, 2560], P(('outer', 'inter'), 'tensor'), may hold values from -0.078125 to 0.078125
Outputs:
- grad_input: bfloat16 [4096, 5120], P(('outer', 'inter'), 'tensor')
- grad_weight: bfloat16 [5120, 2560], P(('outer', 'inter'), 'tensor')
Inputs may be any that keep to these rules, and one draw needn't show every extreme that they name: `storm_index`: each row holds 96 different token positions of one window of 256 tokens.
All inputs are finite; a program needn't handle non-finite values.
Results may differ from a plain program's by a relative error of at most 0.019.
Values may be sent and summed in bfloat16 or wider, within the bound.
A program may use at most 128 MiB of HBM per device.

v0:
```python
import jax
import jax.numpy as jnp
from jax import lax
from jax.sharding import PartitionSpec as P


def local(features, attn_weights, out_grad, storm_index, w_value):
    windows, heads_local, patches, _ = attn_weights.shape
    tokens_local = features.shape[0]
    width_local = out_grad.shape[1]
    head_size = width_local // heads_local
    positions = lax.broadcasted_iota(jnp.int32, (1, 1, patches), 2)
    in_storm = jnp.any(storm_index[:, :, None] == positions, axis=1)
    masked = out_grad.reshape(windows, patches, heads_local, head_size)
    masked = masked * in_storm[:, :, None, None].astype(out_grad.dtype)
    value_grad = jnp.einsum(
        "whij,wihd->wjhd", attn_weights, masked, preferred_element_type=jnp.float32
    )
    value_grad = value_grad.astype(jnp.bfloat16).reshape(tokens_local, width_local)
    outer_count = lax.axis_size("outer")
    pod_sum = lax.psum_scatter(
        lax.dot_general(
            features, value_grad, (((0,), (0,)), ((), ())), preferred_element_type=jnp.float32
        ).astype(jnp.bfloat16),
        "outer",
        scatter_dimension=0,
        tiled=True,
    )
    across = lax.psum_scatter(
        pod_sum.astype(jnp.float32).astype(jnp.bfloat16), "inter", scatter_dimension=0, tiled=True
    ).astype(jnp.float32)
    ranks = outer_count * lax.axis_size("inter")
    grad_weight = (across / ranks).astype(jnp.bfloat16)
    partial_sum = lax.dot_general(
        value_grad,
        lax.all_gather(w_value, ("outer", "inter"), axis=0, tiled=True),
        (((1,), (1,)), ((), ())),
        preferred_element_type=jnp.float32,
    )
    grad_input = lax.psum_scatter(
        partial_sum.astype(jnp.bfloat16), "tensor", scatter_dimension=1, tiled=True
    )
    return (grad_input, grad_weight)


def solution(mesh):
    in_specs = (
        P(("outer", "inter"), None),
        P(("outer", "inter"), "tensor", None, None),
        P(("outer", "inter"), "tensor"),
        P(("outer", "inter"), None),
        P(("outer", "inter"), "tensor"),
    )
    out_specs = (P(("outer", "inter"), "tensor"), P(("outer", "inter"), "tensor"))
    return jax.shard_map(local, mesh=mesh, in_specs=in_specs, out_specs=out_specs, check_vma=False)
```

profile of v0, /device:TPU:0, one launch (start us, length us, event | category | flops | bytes accessed | tf_op | source)
XLA Modules:
  0.0 414.2 jit_solution(7067523243406843978)
XLA Ops:
  8.0 0.0 copy-start
  8.0 0.0 reduce-scatter.8.cloned.1.call-start
  8.1 2.3 copy.13
  10.4 0.7 fusion.4
  11.1 1.9 convolution_convert_fusion.2
  13.0 0.0 copy-done
  13.0 6.6 %fusion = bf16[5120,1280]{0,1:T(8,128)(2,1)} fusion(bf16[256,1280]{0,1:T(8,128)(2,1)S(1)} %bitcast.17, bf16[256,5120]{1,0:T(8,128)(2,1)S(1)} %copy-done), kind=kOutput, calls=%fused_computation.1 | convolution fusion | flops 3361996800 | bytes 16384000 | tf_op jit(solution)/shard_map/dot_general | solution.py:22
  19.6 0.0 reduce-scatter.8.cloned.1.call-update
  19.6 0.0 all-gather.2.cloned.1.call-start
  19.7 0.5 all-gather.2.cloned.1.call-update
  20.2 0.0 reduce-scatter.10.cloned.1.call-start
  20.3 265.2 %reduce-scatter.8.cloned.1.call-done = bf16[1280,1280]{0,1:T(8,128)(2,1)} async-done(((bf16[5120,1280]{0,1:T(8,128)(2,1)}), bf16[1280,1280]{0,1:T(8,128)(2,1)}) %reduce-scatter.8.cloned.1.call-update) | async-done | bytes 3276816 | tf_op jit(solution)/shard_map/reduce_scatter | solution.py:21
  285.5 5.6 %copy.15 = bf16[1280,1280]{1,0:T(8,128)(2,1)} copy(bf16[1280,1280]{0,1:T(8,128)(2,1)} %reduce-scatter.8.cloned.1.call-done) | data formatting | bytes 6553600
  291.1 0.0 reduce-scatter.10.cloned.1.call-update
  291.1 0.0 reduce-scatter.6.cloned.1.call-start
  291.2 92.5 %all-gather.2.cloned.1.call-done = bf16[5120,1280]{1,0:T(8,128)(2,1)} async-done(((bf16[320,1280]{1,0:T(8,128)(2,1)}), bf16[5120,1280]{1,0:T(8,128)(2,1)}) %all-gather.2.cloned.1.call-update) | async-done | bytes 13107216 | tf_op jit(solution)/shard_map/all_gather | solution.py:36
  383.6 14.7 %convolution_convert_fusion.1 = bf16[256,5120]{1,0:T(8,128)(2,1)} fusion(bf16[256,1280]{0,1:T(8,128)(2,1)S(1)} %bitcast.18, bf16[5120,1280]{1,0:T(8,128)(2,1)} %all-gather.2.cloned.1.call-done), kind=kOutput, calls=%fused_computation.2 | convolution fusion | flops 3356753920 | bytes 16384000 | tf_op jit(solution)/shard_map/dot_general | solution.py:34
  398.3 0.0 reduce-scatter.6.cloned.1.call-update
  398.4 0.0 reduce-scatter.10.cloned.1.call-done
  398.4 2.2 copy.16
  400.6 2.3 multiply_convert_fusion
  403.0 2.2 copy.14
  405.2 1.9 reduce-scatter.6.cloned.1.call-done
  (1 shorter events, 0.0 us)
Async XLA Ops:
  8.0 5.0 %copy-start = (bf16[256,5120]{1,0:T(8,128)(2,1)S(1)}, bf16[256,5120]{1,0:T(8,128)(2,1)}, u32[]{:S(2)}) copy-start(bf16[256,5120]{1,0:T(8,128)(2,1)} %param.5) | copy-start | bytes 7864324
  8.0 277.5 %reduce-scatter.8.cloned.1.call-start = ((), (), s32[]{:S(2)}) async-start(), calls=%async_computation.5 | async-start | bytes 16384000 | tf_op jit(solution)/shard_map/reduce_scatter | solution.py:21
  19.6 364.0 %all-gather.2.cloned.1.call-start = ((), (), s32[]{:S(2)}) async-start(), calls=%async_computation.3 | async-start | bytes 13926400 | tf_op jit(solution)/shard_map/all_gather | solution.py:36
  20.2 378.2 %reduce-scatter.10.cloned.1.call-start = ((), (), s32[]{:S(2)}) async-start(), calls=%async_computation.6 | async-start | bytes 4096000
  291.1 116.0 %reduce-scatter.6.cloned.1.call-start = ((), (), s32[]{:S(2)}) async-start(), calls=%async_computation.4 | async-start | bytes 3932160 | tf_op jit(solution)/shard_map/reduce_scatter | solution.py:40
Sparse Core Ops, SparseCore 0:
  19.8 265.7 reduce-scatter.7
  291.3 92.5 reduce-scatter.9
  398.5 8.5 reduce-scatter.5
Sparse Core Ops, SparseCore 1:
  22.9 360.7 all-gather.1
where the time goes:
time: 415 us; the launch traced here: 414 us
  waiting for transfers between devices  360 us (87%)
  matrix products  23.2 us (6%)
  between operations  15.2 us (4%)
  local copies, waits for them, and re-layouts  12.3 us (3%)
    reduce_scatter x1, waiting for transfers between devices, local(): lax.psum_scatter(lax.dot_general(features, value_grad, (((0,), (0,)), (()...  265 us
    all_gather x1, waiting for transfers between devices, local(): lax.all_gather(w_value, ('outer', 'inter'), axis=0, tiled=True)  92.5 us
    dot_general x1, matrix products, local(): lax.dot_general(value_grad, lax.all_gather(w_value, ('outer', 'inter'), a...  14.7 us
    unnamed x6, local copies, waits for them, and re-layouts  12.3 us
  transfers between devices with their start and end apart: 4, of which 3 were waited for; matrix products, arithmetic and copies ran while one was open for 7% of the time, Pallas kernels for 0%

commit v1 on v0

v1 whole, which is shorter than its diff:
```python
import jax
import jax.numpy as jnp
from jax import lax
from jax.sharding import PartitionSpec as P


def shifted(x, axis, count, step):
    if count & (count - 1) == 0:
        pairs = [(k, k ^ step) for k in range(count)]
    else:
        pairs = [(k, (k + step) % count) for k in range(count)]
    return lax.ppermute(x, axis, pairs)


def peer(me, count, step):
    return me ^ step if count & (count - 1) == 0 else (me + step) % count


def origin(me, count, step):
    return me ^ step if count & (count - 1) == 0 else (me - step) % count


def local(features, attn_weights, out_grad, storm_index, w_value):
    windows, heads_local, patches, _ = attn_weights.shape
    tokens = features.shape[0]
    width = out_grad.shape[1]
    head_size = width // heads_local
    rows = w_value.shape[0]
    no, ni, nt = lax.axis_size("outer"), lax.axis_size("inter"), lax.axis_size("tensor")
    me, core = lax.axis_index("inter"), lax.axis_index("tensor")
    half = no // nt
    f32, bf16 = jnp.float32, jnp.bfloat16

    w_all = lax.all_gather(w_value, "outer", axis=0, tiled=True)
    f_view = features.reshape(tokens, no, ni, rows)

    def f_block(i):
        part = lax.dynamic_slice(
            f_view, (0, core * half, i, 0), (tokens, half, 1, rows)
        )
        return part.reshape(tokens, half * rows)

    positions = lax.broadcasted_iota(jnp.int32, (1, 1, patches), 2)
    in_storm = jnp.any(storm_index[:, :, None] == positions, axis=1)
    masked = out_grad.reshape(windows, patches, heads_local, head_size)
    masked = masked * in_storm[:, :, None, None].astype(out_grad.dtype)
    value_grad = jnp.einsum(
        "whij,wihd->wjhd", attn_weights, masked, preferred_element_type=f32
    )
    value_grad = value_grad.astype(bf16).reshape(tokens, width)

    f_parts = [f_block(me)]
    v_parts = [value_grad]
    for step in range(1, ni):
        f_parts.append(shifted(f_block(peer(me, ni, step)), "inter", ni, step))
        v_parts.append(shifted(value_grad, "inter", ni, step))
    v_all = jnp.concatenate(v_parts, axis=0)
    f_mine = jnp.concatenate(f_parts, axis=0)
    ring = [(k, (k + 1) % nt) for k in range(nt)]
    shares = [f_mine]
    for _ in range(1, nt):
        shares.append(lax.ppermute(shares[-1], "tensor", ring))

    term = jnp.zeros((nt, half * rows, width), bf16)
    for back, share in enumerate(shares):
        product = lax.dot_general(
            share, v_all, (((0,), (0,)), ((), ())), preferred_element_type=f32
        ).astype(bf16)
        term = lax.dynamic_update_slice(term, product[None], ((core - back) % nt, 0, 0))
    summed = lax.psum_scatter(
        term.reshape(no * rows, width), "outer", scatter_dimension=0, tiled=True
    )
    grad_weight = (summed.astype(f32) / (no * ni)).astype(bf16)

    part = lax.dot_general(
        v_all, w_all, (((1,), (1,)), ((), ())), preferred_element_type=f32
    ).astype(bf16)
    part = part.reshape(ni * tokens, nt, half * rows)

    def share_of(t):
        return lax.dynamic_slice(
            part, (0, t, 0), (ni * tokens, 1, half * rows)
        ).reshape(ni * tokens, half * rows)

    total = share_of(core).astype(f32)
    for step in range(1, nt):
        pairs = [(k, (k + step) % nt) for k in range(nt)]
        total = total + lax.ppermute(share_of((core + step) % nt), "tensor", pairs).astype(f32)
    total = total.astype(bf16).reshape(ni, tokens, half, rows)
    out = jnp.zeros((tokens, half, ni, rows), bf16)
    for step in range(ni):
        back = (-step) % ni if ni & (ni - 1) else step
        got = total[step] if step == 0 else shifted(total[step], "inter", ni, back)
        source = peer(me, ni, step) if step else me
        out = lax.dynamic_update_slice(out, got[:, :, None, :], (0, 0, source, 0))
    return (out.reshape(tokens, half * ni * rows), grad_weight)


def solution(mesh):
    in_specs = (
        P(("outer", "inter"), None),
        P(("outer", "inter"), "tensor", None, None),
        P(("outer", "inter"), "tensor"),
        P(("outer", "inter"), None),
        P(("outer", "inter"), "tensor"),
    )
    out_specs = (P(("outer", "inter"), "tensor"), P(("outer", "inter"), "tensor"))
    return jax.shard_map(local, mesh=mesh, in_specs=in_specs, out_specs=out_specs, check_vma=False)
```

time: 415 us -> 153 us (0.37)
  waiting for transfers between devices: 360 us -> 75.3 us
  local copies, waits for them, and re-layouts: 12.3 us -> 29.4 us
  starting transfers between devices: 0.16 us -> 11.7 us
  matrix products: 23.2 us -> 17.2 us
    reduce_scatter x2 -> x1, waiting for transfers between devices: 267 us -> 15.3 us  [local(): lax.psum_scatter(term.reshape(no * rows, width), 'outer', scatter_dimensi...]
    all_gather x1, waiting for transfers between devices: 92.5 us -> 0.02 us  [local(): w_all = lax.all_gather(w_value, 'outer', axis=0, tiled=True)]
    ppermute x0 -> x11, waiting for transfers between devices: none -> 59.3 us  [the longest x9 56.3 us: shifted(): return lax.ppermute(x, axis, pairs)]
    ppermute x0 -> x11, starting transfers between devices: none -> 11.7 us  [the longest x9 11.6 us: shifted(): return lax.ppermute(x, axis, pairs)]
    dynamic_slice x0 -> x2, local copies, waits for them, and re-layouts: none -> 10.3 us  [the longest x1 8 us: share_of(): lax.dynamic_slice(part, (0, t, 0), (ni * tokens, 1, half * rows))]
    reshape x0 -> x1, local copies, waits for them, and re-layouts: none -> 6.25 us  [local(): part = part.reshape(ni * tokens, nt, half * rows)]
    unnamed x6 -> x10, local copies, waits for them, and re-layouts: 12.3 us -> 6.46 us
    dot_general x2 -> x3, matrix products: 21.3 us -> 16.9 us  [the longest x2 9.39 us: local(): lax.dot_general(share, v_all, (((0,), (0,)), ((), ())), preferred_element...]
  transfers between devices with their start and end apart: 4 -> 13, of which waited for: 3 -> 9; matrix products, arithmetic and copies ran while one was open for 7% -> 32% of each run, Pallas kernels for 0% -> 0%
where the time goes in v1:
time: 153 us
  waiting for transfers between devices  75.3 us (49%)
  local copies, waits for them, and re-layouts  29.4 us (19%)
  matrix products  17.2 us (11%)
  between operations  14.2 us (9%)
  starting transfers between devices  11.7 us (8%)
  other arithmetic  4.89 us (3%)
    ppermute x9, waiting for transfers between devices, shifted(): return lax.ppermute(x, axis, pairs)  56.3 us
    reduce_scatter x1, waiting for transfers between devices, local(): lax.psum_scatter(term.reshape(no * rows, width), 'outer', scatter_dimensi...  15.3 us
    ppermute x9, starting transfers between devices, shifted(): return lax.ppermute(x, axis, pairs)  11.6 us
    dot_general x2, matrix products, local(): lax.dot_general(share, v_all, (((0,), (0,)), ((), ())), preferred_element...  9.39 us
    dynamic_slice x1, local copies, waits for them, and re-layouts, share_of(): lax.dynamic_slice(part, (0, t, 0), (ni * tokens, 1, half * rows))  8 us
    dot_general x1, matrix products, local(): lax.dot_general(v_all, w_all, (((1,), (1,)), ((), ())), preferred_element...  7.47 us
    unnamed x10, local copies, waits for them, and re-layouts  6.46 us
    reshape x1, local copies, waits for them, and re-layouts, local(): part = part.reshape(ni * tokens, nt, half * rows)  6.25 us
  transfers between devices with their start and end apart: 13, of which 9 were waited for; matrix products, arithmetic and copies ran while one was open for 32% of the time, Pallas kernels for 0%

profile of v1, /device:TPU:0, one launch (start us, length us, event | category | flops | bytes accessed | tf_op | source)
XLA Modules:
  0.0 152.7 jit_solution(8911112731617839318)
XLA Ops:
  7.2 0.0 copy-start
  7.2 0.0 all-gather.2.cloned.1.call-start
  7.2 0.7 all-gather.2.cloned.1.call-update
  7.9 0.0 reduce-scatter.2.cloned.1.call-start
  8.0 4.4 %copy.27 = bf16[256,5120]{0,1:T(8,128)(2,1)} copy(bf16[256,5120]{1,0:T(8,128)(2,1)} %param.5) | data formatting | bytes 5242880 | tf_op args[0]
  12.4 2.3 %constant_dynamic-slice_fusion.3 = (bf16[256,2,1,320]{0,3,2,1:T(8,128)(2,1)S(1)}, bf16[256,2,1,320]{0,3,2,1:T(8,128)(2,1)}, bf16[256,2,1,320]{0,3,2,1:T(8,128)(2,1)}, bf16[256,2,1,320]{0,3,2,1:T(8,128)(2,1)}) fusion(bf16[256,4,4,320]{0,3,2,1:T(8,128)(2,1)} %bitcast.47, s32[]{:T(128)S(6)} %select_n.56, s32[]{:T(128)S(6)} %select_n.52, s32[]{:T(128)S(6)} %select_n.55, ...), kind=kLoop, calls=%fused_computation.26 | loop fusion | bytes 2621460 | tf_op jit(solution)/shard_map/dynamic_slice | solution.py:38
  14.7 3.0 %collective-permute-start.7 = (bf16[256,640]{0,1:T(8,128)(2,1)}, bf16[256,640]{0,1:T(8,128)(2,1)S(1)}, u32[]{:S(2)}, u32[]{:S(2)}) collective-permute-start(bf16[256,640]{0,1:T(8,128)(2,1)} %bitcast.21), channel_id=1, source_target_pairs={{0,1},{1,0},{2,3},{3,2},{4,5},{5,4},{6,7},{7,6},{8,9},{9,8},{10,11... | collective-permute-start | bytes 983048 | tf_op jit(solution)/shard_map/ppermute | solution.py:12
  17.7 1.5 collective-permute-start.8
  19.2 0.2 copy.19
  19.4 0.1 fusion.8
  19.6 6.9 %collective-permute-done.7 = bf16[256,640]{0,1:T(8,128)(2,1)S(1)} collective-permute-done((bf16[256,640]{0,1:T(8,128)(2,1)}, bf16[256,640]{0,1:T(8,128)(2,1)S(1)}, u32[]{:S(2)}, u32[]{:S(2)}) %collective-permute-start.7) | collective-permute-done | bytes 327712 | tf_op jit(solution)/shard_map/ppermute | solution.py:12
  26.4 7.7 %collective-permute-done.8 = bf16[256,640]{0,1:T(8,128)(2,1)} collective-permute-done((bf16[256,640]{0,1:T(8,128)(2,1)}, bf16[256,640]{0,1:T(8,128)(2,1)}, u32[]{:S(2)}, u32[]{:S(2)}) %collective-permute-start.8) | collective-permute-done | bytes 327712 | tf_op jit(solution)/shard_map/ppermute | solution.py:12
  34.2 2.3 %pad_maximum_fusion.1 = bf16[1024,640]{0,1:T(8,128)(2,1)} fusion(bf16[256,640]{0,1:T(8,128)(2,1)} %collective-permute-done.9, bf16[256,640]{0,1:T(8,128)(2,1)} %collective-permute-done.8, bf16[256,640]{0,1:T(8,128)(2,1)S(1)} %collective-permute-done.7, bf16[256,640]{0,1:T(8,128)(2,1)S(1)} %bitcast.50), kind=kLoop, calls=%fused_computation.12 | loop fusion | flops 5242880 | bytes 2621440 | tf_op jit(solution)/shard_map/concatenate | solution.py:58
  36.5 0.4 convolution_convert_fusion.3
  36.9 1.3 collective-permute-start
  38.2 0.8 collective-permute-start.1
  39.0 1.4 collective-permute-start.2
  40.4 14.1 %collective-permute-done = bf16[256,1280]{0,1:T(8,128)(2,1)S(1)} collective-permute-done((bf16[256,1280]{0,1:T(8,128)(2,1)S(1)}, bf16[256,1280]{0,1:T(8,128)(2,1)S(1)}, u32[]{:S(2)}, u32[]{:S(2)}) %collective-permute-start) | collective-permute-done | bytes 655392 | tf_op jit(solution)/shard_map/ppermute | solution.py:12
  54.5 12.9 %collective-permute-done.1 = bf16[256,1280]{0,1:T(8,128)(2,1)} collective-permute-done((bf16[256,1280]{0,1:T(8,128)(2,1)S(1)}, bf16[256,1280]{0,1:T(8,128)(2,1)}, u32[]{:S(2)}, u32[]{:S(2)}) %collective-permute-start.1) | collective-permute-done | bytes 655392 | tf_op jit(solution)/shard_map/ppermute | solution.py:12
  67.4 1.7 %collective-permute-done.2 = bf16[256,1280]{0,1:T(8,128)(2,1)} collective-permute-done((bf16[256,1280]{0,1:T(8,128)(2,1)S(1)}, bf16[256,1280]{0,1:T(8,128)(2,1)}, u32[]{:S(2)}, u32[]{:S(2)}) %collective-permute-start.2) | collective-permute-done | bytes 655392 | tf_op jit(solution)/shard_map/ppermute | solution.py:12
  69.2 1.9 %broadcast_in_dim.27 = bf16[2,640,1280]{2,1,0:T(8,128)(2,1)} broadcast(bf16[]{:T(256)} %constant.35.clone.1), dimensions={} | broadcast | bytes 3276802 | tf_op jit(solution)/shard_map/broadcast_in_dim | solution.py:64
  71.1 4.6 %fusion.1 = bf16[2,640,1280]{2,1,0:T(8,128)(2,1)} fusion(bf16[2,640,1280]{2,1,0:T(8,128)(2,1)} %broadcast_in_dim.27, s32[]{:T(128)S(6)} %select_n.58, bf16[256,640]{0,1:T(8,128)(2,1)} %collective-permute-done.9, bf16[256,640]{0,1:T(8,128)(2,1)} %collective-permute-done.8, bf16[256,640]{0,1:T(8,128)(2,1)S(1)} %collective-permute-done.7, ...), kind=kOutput, calls=%fused_computation.4 | convolution fusion | flops 1694269440 | bytes 5570564 | tf_op jit(solution)/shard_map/dot_general | solution.py:66
  75.7 4.8 %fusion.3 = bf16[2,640,1280]{2,1,0:T(8,128)(2,1)} fusion(bf16[2,640,1280]{2,1,0:T(8,128)(2,1)} %fusion.1, s32[]{:T(128)S(6)} %select_n.60, bf16[1024,640]{0,1:T(8,128)(2,1)} %collective-permute-done.10, bf16[256,1280]{0,1:T(8,128)(2,1)} %collective-permute-done.2, bf16[256,1280]{0,1:T(8,128)(2,1)} %collective-permute-done.1, ...), kind=kOutput, calls=%fused_computation.6 | convolution fusion | flops 1689026560 | bytes 5570564 | tf_op jit(solution)/shard_map/dot_general | solution.py:66
  80.5 0.0 reduce-scatter.2.cloned.1.call-update
  80.6 0.0 all-gather.2.cloned.1.call-done
  80.6 7.5 %convolution_convert_fusion = bf16[1024,1280]{1,0:T(8,128)(2,1)} fusion(bf16[1280,1280]{1,0:T(8,128)(2,1)} %all-gather.2.cloned.1.call-done, bf16[256,1280]{0,1:T(8,128)(2,1)} %collective-permute-done.2, bf16[256,1280]{0,1:T(8,128)(2,1)} %collective-permute-done.1, bf16[256,1280]{0,1:T(8,128)(2,1)S(1)} %collective-permute-done, bf16[256,1280]{0,1:T(8,128)(2,1)S(1)} %bitcast.59), kind=kOutput, calls=%fused_computation | convolution fusion | flops 3367239680 | bytes 8519680 | tf_op jit(solution)/shard_map/dot_general | solution.py:75
  88.1 6.3 %reshape.110 = bf16[1024,2,640]{2,1,0:T(2,128)(2,1)} reshape(bf16[1024,1280]{1,0:T(8,128)(2,1)} %convolution_convert_fusion) | data formatting | bytes 5242880 | tf_op jit(solution)/shard_map/reshape | solution.py:78
  94.3 8.0 %constant_dynamic-slice_fusion.5 = (bf16[1024,1,640]{2,1,0:T(2,128)(2,1)S(1)}, bf16[1024,1,640]{2,1,0:T(2,128)(2,1)S(1)}) fusion(bf16[1024,2,640]{2,1,0:T(2,128)(2,1)} %reshape.110, s32[]{:T(128)S(6)} %select_n.49, s32[]{:T(128)S(6)} %select_n.51), kind=kLoop, calls=%fused_computation.29 | loop fusion | bytes 5242888 | tf_op jit(solution)/shard_map/dynamic_slice | solution.py:81
  102.3 0.2 copy.35
  102.5 0.1 collective-permute-start.3
  102.6 3.0 %collective-permute-done.3 = bf16[1024,640]{1,0:T(8,128)(2,1)S(1)} collective-permute-done((bf16[1024,640]{1,0:T(8,128)(2,1)S(1)}, bf16[1024,640]{1,0:T(8,128)(2,1)S(1)}, u32[]{:S(2)}, u32[]{:S(2)}) %collective-permute-start.3) | collective-permute-done | bytes 1310752 | tf_op jit(solution)/shard_map/ppermute | solution.py:88
  105.6 0.3 fusion.4
  106.0 0.1 fusion.9
  106.1 0.9 copy.24
  107.0 0.9 collective-permute-start.4
  107.9 0.2 copy.22
  108.1 0.9 copy.25
  109.0 1.5 collective-permute-start.5
  110.5 0.2 copy.26
  110.7 1.1 collective-permute-start.6
  111.8 0.1 broadcast_in_dim.23
  111.9 5.9 %collective-permute-done.4 = bf16[256,2,320]{0,2,1:T(8,128)(2,1)} collective-permute-done((bf16[256,2,320]{0,2,1:T(8,128)(2,1)}, bf16[256,2,320]{0,2,1:T(8,128)(2,1)}, u32[]{:S(2)}, u32[]{:S(2)}) %collective-permute-start.4) | collective-permute-done | bytes 327712 | tf_op jit(solution)/shard_map/ppermute | solution.py:12
  117.9 1.0 bitcast_dynamic-update-slice_fusion.2
  118.9 6.9 %collective-permute-done.5 = bf16[256,2,320]{0,2,1:T(8,128)(2,1)} collective-permute-done((bf16[256,2,320]{0,2,1:T(8,128)(2,1)}, bf16[256,2,320]{0,2,1:T(8,128)(2,1)}, u32[]{:S(2)}, u32[]{:S(2)}) %collective-permute-start.5) | collective-permute-done | bytes 327712 | tf_op jit(solution)/shard_map/ppermute | solution.py:12
  125.8 1.0 bitcast_dynamic-update-slice_fusion.1
  126.8 1.6 %copy.28 = bf16[256,2560]{1,0:T(8,128)(2,1)} copy(bf16[256,2560]{0,1:T(8,128)(2,1)S(1)} %bitcast.48) | data formatting | bytes 2621440
  128.4 15.3 %reduce-scatter.2.cloned.1.call-done = bf16[320,1280]{1,0:T(8,128)(2,1)} async-done(((bf16[1280,1280]{1,0:T(8,128)(2,1)}), bf16[320,1280]{1,0:T(8,128)(2,1)}) %reduce-scatter.2.cloned.1.call-update) | async-done | bytes 819216 | tf_op jit(solution)/shard_map/reduce_scatter | solution.py:70
  143.7 2.2 %multiply_convert_fusion = bf16[320,1280]{1,0:T(8,128)(2,1)} fusion(bf16[320,1280]{1,0:T(8,128)(2,1)} %reduce-scatter.2.cloned.1.call-done), kind=kLoop, calls=%fused_computation.10 | loop fusion | flops 1228800 | bytes 1638400 | tf_op jit(solution)/shard_map/convert_element_type | solution.py:73
  (13 shorter events, 0.1 us)
Async XLA Ops:
  7.2 29.3 %copy-start = (bf16[1,10,256,256]{3,2,1,0:T(8,128)(2,1)S(1)}, bf16[1,10,256,256]{3,2,1,0:T(8,128)(2,1)}, u32[]{:S(2)}) copy-start(bf16[1,10,256,256]{3,2,1,0:T(8,128)(2,1)} %param.6) | copy-start | bytes 3932164
  7.2 73.4 %all-gather.2.cloned.1.call-start = ((), (), s32[]{:S(2)}) async-start(), calls=%async_computation.1 | async-start | bytes 4096000 | tf_op jit(solution)/shard_map/all_gather | solution.py:34
  7.9 135.8 %reduce-scatter.2.cloned.1.call-start = ((), (), s32[]{:S(2)}) async-start(), calls=%async_computation.2 | async-start | bytes 4096000 | tf_op jit(solution)/shard_map/reduce_scatter | solution.py:70
  12.4 6.8 %copy-start.1 = (bf16[256,1280]{1,0:T(8,128)(2,1)S(1)}, bf16[256,1280]{1,0:T(8,128)(2,1)}, u32[]{:S(2)}) copy-start(bf16[256,1280]{1,0:T(8,128)(2,1)} %param.7) | copy-start | bytes 1966084
  12.4 7.0 %copy-start.2 = (s32[1,96]{1,0:T(1,128)S(1)}, s32[1,96]{1,0:T(1,128)}, u32[]{:S(2)}) copy-start(s32[1,96]{1,0:T(1,128)} %param.8) | copy-start | bytes 1156
  14.7 11.7 %collective-permute-start.7 = (bf16[256,640]{0,1:T(8,128)(2,1)}, bf16[256,640]{0,1:T(8,128)(2,1)S(1)}, u32[]{:S(2)}, u32[]{:S(2)}) collective-permute-start(bf16[256,640]{0,1:T(8,128)(2,1)} %bitcast.21), channel_id=1, source_target_pairs={{0,1},{1,0},{2,3},{3,2},{4,5},{5,4},{6,7},{7,6},{8,9},{9,8},{10,11... | collective-permute-start | bytes 983048 | tf_op jit(solution)/shard_map/ppermute | solution.py:12
  17.7 16.5 %collective-permute-start.8 = (bf16[256,640]{0,1:T(8,128)(2,1)}, bf16[256,640]{0,1:T(8,128)(2,1)}, u32[]{:S(2)}, u32[]{:S(2)}) collective-permute-start(bf16[256,640]{0,1:T(8,128)(2,1)} %bitcast.22), channel_id=1, source_target_pairs={{0,2},{1,3},{2,0},{3,1},{4,6},{5,7},{6,4},{7,5},{8,10},{9,11},{10,... | collective-permute-start | bytes 983048 | tf_op jit(solution)/shard_map/ppermute | solution.py:12
  19.2 15.0 %collective-permute-start.9 = (bf16[256,640]{0,1:T(8,128)(2,1)}, bf16[256,640]{0,1:T(8,128)(2,1)}, u32[]{:S(2)}, u32[]{:S(2)}) collective-permute-start(bf16[256,640]{0,1:T(8,128)(2,1)} %bitcast.23), channel_id=1, source_target_pairs={{0,3},{1,2},{2,1},{3,0},{4,7},{5,6},{6,5},{7,4},{8,11},{9,10},{10,... | collective-permute-start | bytes 983048 | tf_op jit(solution)/shard_map/ppermute | solution.py:12
  36.5 39.2 %collective-permute-start.10 = (bf16[1024,640]{0,1:T(8,128)(2,1)}, bf16[1024,640]{0,1:T(8,128)(2,1)}, u32[]{:S(2)}, u32[]{:S(2)}) collective-permute-start(bf16[1024,640]{0,1:T(8,128)(2,1)} %pad_maximum_fusion.1), channel_id=1, source_target_pairs={{0,16},{16,0},{1,17},{17,1},{2,18},{18,2},{3,19},{19,3},{4,20},{20... | collective-permute-start | bytes 3932168 | tf_op jit(solution)/shard_map/ppermute | solution.py:62
  36.9 17.7 %collective-permute-start = (bf16[256,1280]{0,1:T(8,128)(2,1)S(1)}, bf16[256,1280]{0,1:T(8,128)(2,1)S(1)}, u32[]{:S(2)}, u32[]{:S(2)}) collective-permute-start(bf16[256,1280]{0,1:T(8,128)(2,1)S(1)} %bitcast.54), channel_id=1, source_target_pairs={{0,1},{1,0},{2,3},{3,2},{4,5},{5,4},{6,7},{7,6},{8,9},{9,8},{10,11... | collective-permute-start | bytes 1966088 | tf_op jit(solution)/shard_map/ppermute | solution.py:12
  38.2 29.3 %collective-permute-start.1 = (bf16[256,1280]{0,1:T(8,128)(2,1)S(1)}, bf16[256,1280]{0,1:T(8,128)(2,1)}, u32[]{:S(2)}, u32[]{:S(2)}) collective-permute-start(bf16[256,1280]{0,1:T(8,128)(2,1)S(1)} %bitcast.55), channel_id=1, source_target_pairs={{0,2},{1,3},{2,0},{3,1},{4,6},{5,7},{6,4},{7,5},{8,10},{9,11},{10,... | collective-permute-start | bytes 1966088 | tf_op jit(solution)/shard_map/ppermute | solution.py:12
  39.0 30.2 %collective-permute-start.2 = (bf16[256,1280]{0,1:T(8,128)(2,1)S(1)}, bf16[256,1280]{0,1:T(8,128)(2,1)}, u32[]{:S(2)}, u32[]{:S(2)}) collective-permute-start(bf16[256,1280]{0,1:T(8,128)(2,1)S(1)} %bitcast.56), channel_id=1, source_target_pairs={{0,3},{1,2},{2,1},{3,0},{4,7},{5,6},{6,5},{7,4},{8,11},{9,10},{10,... | collective-permute-start | bytes 1966088 | tf_op jit(solution)/shard_map/ppermute | solution.py:12
  102.5 3.1 %collective-permute-start.3 = (bf16[1024,640]{1,0:T(8,128)(2,1)S(1)}, bf16[1024,640]{1,0:T(8,128)(2,1)S(1)}, u32[]{:S(2)}, u32[]{:S(2)}) collective-permute-start(bf16[1024,640]{1,0:T(8,128)(2,1)S(1)} %bitcast.53), channel_id=1, source_target_pairs={{0,16},{16,0},{1,17},{17,1},{2,18},{18,2},{3,19},{19,3},{4,20},{20... | collective-permute-start | bytes 3932168 | tf_op jit(solution)/shard_map/ppermute | solution.py:88
  107.0 10.9 %collective-permute-start.4 = (bf16[256,2,320]{0,2,1:T(8,128)(2,1)}, bf16[256,2,320]{0,2,1:T(8,128)(2,1)}, u32[]{:S(2)}, u32[]{:S(2)}) collective-permute-start(bf16[256,2,320]{0,2,1:T(8,128)(2,1)} %bitcast.12), channel_id=1, source_target_pairs={{0,1},{1,0},{2,3},{3,2},{4,5},{5,4},{6,7},{7,6},{8,9},{9,8},{10,11... | collective-permute-start | bytes 983048 | tf_op jit(solution)/shard_map/ppermute | solution.py:12
  109.0 16.8 %collective-permute-start.5 = (bf16[256,2,320]{0,2,1:T(8,128)(2,1)}, bf16[256,2,320]{0,2,1:T(8,128)(2,1)}, u32[]{:S(2)}, u32[]{:S(2)}) collective-permute-start(bf16[256,2,320]{0,2,1:T(8,128)(2,1)} %bitcast.14), channel_id=1, source_target_pairs={{0,2},{1,3},{2,0},{3,1},{4,6},{5,7},{6,4},{7,5},{8,10},{9,11},{10,... | collective-permute-start | bytes 983048 | tf_op jit(solution)/shard_map/ppermute | solution.py:12
  110.7 16.1 %collective-permute-start.6 = (bf16[256,2,320]{0,2,1:T(8,128)(2,1)S(1)}, bf16[256,2,320]{0,2,1:T(8,128)(2,1)S(1)}, u32[]{:S(2)}, u32[]{:S(2)}) collective-permute-start(bf16[256,2,320]{0,2,1:T(8,128)(2,1)S(1)} %bitcast.60), channel_id=1, source_target_pairs={{0,3},{1,2},{2,1},{3,0},{4,7},{5,6},{6,5},{7,4},{8,11},{9,10},{10,... | collective-permute-start | bytes 983048 | tf_op jit(solution)/shard_map/ppermute | solution.py:12
Sparse Core Ops, SparseCore 0:
  9.6 68.3 all-gather.1
  80.7 62.9 reduce-scatter.1

commit v2 on v1

v2 whole, which is shorter than its diff:
```python
import jax
import jax.numpy as jnp
from jax import lax
from jax.sharding import PartitionSpec as P


def shifted(x, axis, count, step):
    if count & (count - 1) == 0:
        pairs = [(k, k ^ step) for k in range(count)]
    else:
        pairs = [(k, (k + step) % count) for k in range(count)]
    return lax.ppermute(x, axis, pairs)


def peer(me, count, step):
    return me ^ step if count & (count - 1) == 0 else (me + step) % count


def local(features, attn_weights, out_grad, storm_index, w_value):
    windows, heads_local, patches, _ = attn_weights.shape
    tokens = features.shape[0]
    width = out_grad.shape[1]
    head_size = width // heads_local
    rows = w_value.shape[0]
    no, ni, nt = lax.axis_size("outer"), lax.axis_size("inter"), lax.axis_size("tensor")
    me, core, place = lax.axis_index("inter"), lax.axis_index("tensor"), lax.axis_index("outer")
    half = no // nt
    f32, bf16 = jnp.float32, jnp.bfloat16

    positions = lax.broadcasted_iota(jnp.int32, (1, 1, patches), 2)
    in_storm = jnp.any(storm_index[:, :, None] == positions, axis=1)
    masked = out_grad.reshape(windows, patches, heads_local, head_size)
    masked = masked * in_storm[:, :, None, None].astype(out_grad.dtype)
    value_grad = jnp.einsum(
        "whij,wihd->wjhd", attn_weights, masked, preferred_element_type=f32
    )
    value_grad = value_grad.astype(bf16).reshape(tokens, width)

    value_grad, features = lax.optimization_barrier((value_grad, features))

    if ni == 4:
        cut = width // 2
        v_one = shifted(value_grad, "inter", ni, 1)
        v_two = shifted(value_grad, "inter", ni, 2)
        far_a = shifted(v_one[:, :cut], "inter", ni, 2)
        far_b = shifted(v_two[:, cut:], "inter", ni, 1)
        v_far = jnp.concatenate([far_a, far_b], axis=1)
        v_parts = [value_grad, v_one, v_two, v_far]
    else:
        v_parts = [value_grad] + [shifted(value_grad, "inter", ni, s) for s in range(1, ni)]
    v_all = jnp.concatenate(v_parts, axis=0)

    f_view = features.reshape(tokens, no, ni, rows)

    def f_block(i):
        part = lax.dynamic_slice(
            f_view, (0, core * half, i, 0), (tokens, half, 1, rows)
        )
        return part.reshape(tokens, half * rows)

    ups, downs = [w_value], [w_value]

    def hop_on(hop):
        right = [(k, k + 1) for k in range(hop - 1, no - 1)]
        left = [(k, k - 1) for k in range(1, no - hop + 1)]
        ups.append(lax.ppermute(ups[-1], "outer", right))
        downs.append(lax.ppermute(downs[-1], "outer", left))

    hop_on(1)
    ups[1], downs[1], _ = lax.optimization_barrier((ups[1], downs[1], v_parts[1]))
    hop_on(2)

    f_parts = [f_block(me)] + [f_block(peer(me, ni, step)) for step in range(1, ni)]
    f_parts, _ = lax.optimization_barrier((f_parts, v_parts[1:3]))
    for step in range(1, ni):
        f_parts[step] = shifted(f_parts[step], "inter", ni, step)
    f_parts, _ = lax.optimization_barrier((f_parts, ups[1:2] + downs[1:2]))
    f_mine = jnp.concatenate(f_parts, axis=0)
    ring = [(k, (k + 1) % nt) for k in range(nt)]
    shares = [f_mine]
    for _ in range(1, nt):
        shares.append(lax.ppermute(shares[-1], "tensor", ring))
    ups[2], downs[2], _ = lax.optimization_barrier((ups[2], downs[2], shares[0]))
    for hop in range(3, no):
        hop_on(hop)
    pieces = []
    for t in range(nt):
        piece = shares[0]
        for back in range(1, nt):
            piece = jnp.where((core - back) % nt == t, shares[back], piece)
        pieces.append(piece)
    f_all = jnp.concatenate(pieces, axis=1)

    term = lax.dot_general(
        f_all, v_all, (((0,), (0,)), ((), ())), preferred_element_type=f32
    ).astype(bf16).reshape(no, rows, width)

    ups[-1], downs[-1], _ = lax.optimization_barrier((ups[-1], downs[-1], term))
    w_all = jnp.zeros((no, rows, width), bf16)
    for hop in range(no):
        block = w_value if hop == 0 else jnp.where(place >= hop, ups[hop], downs[no - hop])
        w_all = lax.dynamic_update_slice(w_all, block[None], ((place - hop) % no, 0, 0))

    def block_of(o):
        return lax.dynamic_index_in_dim(term, jnp.clip(o, 0, no - 1), 0, keepdims=False)

    up, down = None, None
    for step in range(no - 1):
        add_up, add_down = block_of(place + no - 1 - step), block_of(place - no + 1 + step)
        if step:
            add_up = (up.astype(f32) + add_up.astype(f32)).astype(bf16)
            add_down = (down.astype(f32) + add_down.astype(f32)).astype(bf16)
        up = lax.ppermute(add_up, "outer", [(k, k + 1) for k in range(min(step + 1, no - 1))])
        down = lax.ppermute(
            add_down, "outer", [(k, k - 1) for k in range(max(1, no - 1 - step), no)]
        )
    summed = block_of(place).astype(f32) + up.astype(f32) + down.astype(f32)
    grad_weight = (summed / (no * ni)).astype(bf16)

    def share_of(t):
        w_share = lax.dynamic_slice(w_all, (t * half, 0, 0), (half, rows, width))
        return lax.dot_general(
            v_all,
            w_share.reshape(half * rows, width),
            (((1,), (1,)), ((), ())),
            preferred_element_type=f32,
        ).astype(bf16)

    total = 0.0
    for step in list(range(1, nt)) + [0]:
        share = share_of((core + step) % nt)
        if step:
            share = lax.ppermute(share, "tensor", [(k, (k + step) % nt) for k in range(nt)])
        total = total + share.astype(f32)
    total = total.astype(bf16).reshape(ni, tokens, half, rows)
    out = jnp.zeros((tokens, half, ni, rows), bf16)
    for step in range(ni):
        back = (-step) % ni if ni & (ni - 1) else step
        got = total[step] if step == 0 else shifted(total[step], "inter", ni, back)
        source = peer(me, ni, step) if step else me
        out = lax.dynamic_update_slice(out, got[:, :, None, :], (0, 0, source, 0))
    return (out.reshape(tokens, half * ni * rows), grad_weight)


def solution(mesh):
    in_specs = (
        P(("outer", "inter"), None),
        P(("outer", "inter"), "tensor", None, None),
        P(("outer", "inter"), "tensor"),
        P(("outer", "inter"), None),
        P(("outer", "inter"), "tensor"),
    )
    out_specs = (P(("outer", "inter"), "tensor"), P(("outer", "inter"), "tensor"))

    return jax.shard_map(local, mesh=mesh, in_specs=in_specs, out_specs=out_specs, check_vma=False)
```

time: 153 us -> 157 us (1.026)
  starting transfers between devices: 11.7 us -> 45.8 us
  waiting for transfers between devices: 75.3 us -> 61.7 us
  between operations: 14.2 us -> 1.13 us
  local copies, waits for them, and re-layouts: 29.4 us -> 17.3 us
  other arithmetic: 4.89 us -> 15.1 us
  matrix products: 17.2 us -> 15.4 us
    ppermute x1 -> x13, waiting for transfers between devices: 3.02 us -> 50.6 us  [the longest x3 29.1 us: hop_on(): downs.append(lax.ppermute(downs[-1], 'outer', left))]
    ppermute x9 -> x10, waiting for transfers between devices: 56.3 us -> 11 us  [shifted(): return lax.ppermute(x, axis, pairs)]
    ppermute x1 -> x13, starting transfers between devices: 0.07 us -> 32.1 us  [the longest x3 18 us: local(): lax.ppermute(add_up, 'outer', [(k, k + 1) for k in range(min(step + 1, no...]
    reduce_scatter x1 -> x0, waiting for transfers between devices: 15.3 us -> none  [local(): lax.psum_scatter(term.reshape(no * rows, width), 'outer', scatter_dimensi...]
    dynamic_slice x1, local copies, waits for them, and re-layouts: 8 us -> 0.22 us  [share_of(): w_share = lax.dynamic_slice(w_all, (t * half, 0, 0), (half, rows, width))]
    convert_element_type x2 -> x3, other arithmetic: 2.48 us -> 9.76 us  [the longest x2 6.88 us: local(): add_up = (up.astype(f32) + add_up.astype(f32)).astype(bf16)]
    reshape x1 -> x0, local copies, waits for them, and re-layouts: 6.25 us -> none  [local(): part = part.reshape(ni * tokens, nt, half * rows)]
    optimization_barrier x0 -> x1, local copies, waits for them, and re-layouts: none -> 4.39 us  [local(): value_grad, features = lax.optimization_barrier((value_grad, features))]
  transfers between devices with their start and end apart: 13 -> 24, of which waited for: 9 -> 12; matrix products, arithmetic and copies ran while one was open for 32% -> 26% of each run, Pallas kernels for 0% -> 0%
where the time goes in v2:
time: 157 us; the launch traced here: 156 us
  waiting for transfers between devices  61.7 us (39%)
  starting transfers between devices  45.8 us (29%)
  local copies, waits for them, and re-layouts  17.3 us (11%)
  matrix products  15.4 us (10%)
  other arithmetic  15.1 us (10%)
    ppermute x3, waiting for transfers between devices, hop_on(): downs.append(lax.ppermute(downs[-1], 'outer', left))  29.1 us
    ppermute x3, starting transfers between devices, local(): lax.ppermute(add_up, 'outer', [(k, k + 1) for k in range(min(step + 1, no...  18 us
    ppermute x3, waiting for transfers between devices, local(): lax.ppermute(add_up, 'outer', [(k, k + 1) for k in range(min(step + 1, no...  14.6 us
    ppermute x10, starting transfers between devices, shifted(): return lax.ppermute(x, axis, pairs)  13.6 us
    ppermute x10, waiting for transfers between devices, shifted(): return lax.ppermute(x, axis, pairs)  11 us
    dot_general x2, matrix products, share_of(): lax.dot_general(v_all, w_share.reshape(half * rows, width), (((1,), (1,))...  8.97 us
    convert_element_type x2, other arithmetic, local(): add_up = (up.astype(f32) + add_up.astype(f32)).astype(bf16)  6.88 us
    ppermute x3, starting transfers between devices, hop_on(): ups.append(lax.ppermute(ups[-1], 'outer', right))  5.83 us
  transfers between devices with their start and end apart: 24, of which 12 were waited for; matrix products, arithmetic and copies ran while one was open for 26% of the time, Pallas kernels for 0%

profile of v2, /device:TPU:0, one launch (start us, length us, event | category | flops | bytes accessed | tf_op | source)
XLA Modules:
  0.0 156.4 jit_solution(12458181931913472489)
XLA Ops:
  0.7 1.5 copy.25
  2.9 1.2 convolution_convert_fusion.3
  4.1 3.0 %collective-permute-start = (bf16[256,1280]{0,1:T(8,128)(2,1)}, bf16[256,1280]{0,1:T(8,128)(2,1)}, u32[]{:S(2)}, u32[]{:S(2)}) collective-permute-start(bf16[256,1280]{0,1:T(8,128)(2,1)} %bitcast.5), channel_id=1, source_target_pairs={{0,1},{1,0},{2,3},{3,2},{4,5},{5,4},{6,7},{7,6},{8,9},{9,8},{10,11... | collective-permute-start | bytes 1966088 | tf_op jit(solution)/shard_map/ppermute | solution.py:12
  7.1 1.5 collective-permute-start.1
  8.6 3.5 %collective-permute-start.4 = (bf16[320,1280]{1,0:T(8,128)(2,1)S(1)}, bf16[320,1280]{1,0:T(8,128)(2,1)S(1)}, u32[]{:S(2)}, u32[]{:S(2)}) collective-permute-start(bf16[320,1280]{1,0:T(8,128)(2,1)S(1)} %copy-done.2), channel_id=1, source_target_pairs={{0,4},{4,8},{8,12},{1,5},{5,9},{9,13},{2,6},{6,10},{10,14},{3,7},{... | collective-permute-start | bytes 2457608 | tf_op jit(solution)/shard_map/ppermute | solution.py:66
  12.2 1.3 collective-permute-start.5
  13.5 4.4 %copy.26 = bf16[256,5120]{0,1:T(8,128)(2,1)} copy(bf16[256,5120]{1,0:T(8,128)(2,1)} %param.5) | data formatting | bytes 5242880 | tf_op jit(solution)/shard_map/optimization_barrier | solution.py:39
  17.9 1.4 constant_dynamic-slice_fusion.2
  19.2 2.9 %collective-permute-done = bf16[256,1280]{0,1:T(8,128)(2,1)} collective-permute-done((bf16[256,1280]{0,1:T(8,128)(2,1)}, bf16[256,1280]{0,1:T(8,128)(2,1)}, u32[]{:S(2)}, u32[]{:S(2)}) %collective-permute-start) | collective-permute-done | bytes 655392 | tf_op jit(solution)/shard_map/ppermute | solution.py:12
  22.2 1.5 collective-permute-done.1
  23.6 1.5 collective-permute-start.10
  25.1 1.5 collective-permute-start.8
  27.1 1.9 %collective-permute-done.4 = bf16[320,1280]{1,0:T(8,128)(2,1)S(1)} collective-permute-done((bf16[320,1280]{1,0:T(8,128)(2,1)S(1)}, bf16[320,1280]{1,0:T(8,128)(2,1)S(1)}, u32[]{:S(2)}, u32[]{:S(2)}) %collective-permute-start.4) | collective-permute-done | bytes 819232 | tf_op jit(solution)/shard_map/ppermute | solution.py:66
  29.0 4.3 %collective-permute-done.5 = bf16[320,1280]{1,0:T(8,128)(2,1)} collective-permute-done((bf16[320,1280]{1,0:T(8,128)(2,1)S(1)}, bf16[320,1280]{1,0:T(8,128)(2,1)}, u32[]{:S(2)}, u32[]{:S(2)}) %collective-permute-start.5) | collective-permute-done | bytes 819232 | tf_op jit(solution)/shard_map/ppermute | solution.py:67
  33.3 1.8 %collective-permute-done.10 = bf16[256,640]{0,1:T(8,128)(2,1)S(1)} collective-permute-done((bf16[256,640]{0,1:T(8,128)(2,1)S(1)}, bf16[256,640]{0,1:T(8,128)(2,1)S(1)}, u32[]{:S(2)}, u32[]{:S(2)}) %collective-permute-start.10) | collective-permute-done | bytes 327712 | tf_op jit(solution)/shard_map/ppermute | solution.py:12
  35.1 4.8 %collective-permute-done.8 = bf16[256,640]{0,1:T(8,128)(2,1)S(1)} collective-permute-done((bf16[256,640]{0,1:T(8,128)(2,1)S(1)}, bf16[256,640]{0,1:T(8,128)(2,1)S(1)}, u32[]{:S(2)}, u32[]{:S(2)}) %collective-permute-start.8) | collective-permute-done | bytes 327712 | tf_op jit(solution)/shard_map/ppermute | solution.py:12
  40.2 1.6 %collective-permute-start.6 = (bf16[320,1280]{1,0:T(8,128)(2,1)}, bf16[320,1280]{1,0:T(8,128)(2,1)}, u32[]{:S(2)}, u32[]{:S(2)}) collective-permute-start(bf16[320,1280]{1,0:T(8,128)(2,1)} %copy-done.3), channel_id=1, source_target_pairs={{4,8},{8,12},{5,9},{9,13},{6,10},{10,14},{7,11},{11,15},{20,24},{2... | collective-permute-start | bytes 2457608 | tf_op jit(solution)/shard_map/ppermute | solution.py:66
  41.8 1.3 collective-permute-start.7
  43.5 1.0 slice.28
  44.5 1.5 collective-permute-start.2
  47.6 19.4 %collective-permute-done.7 = bf16[320,1280]{1,0:T(8,128)(2,1)} collective-permute-done((bf16[320,1280]{1,0:T(8,128)(2,1)}, bf16[320,1280]{1,0:T(8,128)(2,1)}, u32[]{:S(2)}, u32[]{:S(2)}) %collective-permute-start.7) | collective-permute-done | bytes 819232 | tf_op jit(solution)/shard_map/ppermute | solution.py:67
  67.7 1.3 collective-permute-start.12
  69.1 1.5 broadcast_select_fusion.1
  70.6 5.2 %convolution_convert_fusion = bf16[1280,1280]{1,0:T(8,128)(2,1)S(1)} fusion(bf16[1024,640]{0,1:T(8,128)(2,1)S(1)} %get-tuple-element.47, bf16[1024,640]{0,1:T(8,128)(2,1)S(1)} %get-tuple-element.46, bf16[256,640]{0,1:T(8,128)(2,1)S(1)} %collective-permute-done.3, bf16[256,640]{0,1:T(8,128)(2,1)S(1)} %collective-permute-done.2, ...), kind=kOutput, calls=%fused_computation | convolution fusion | flops 3375431680 | bytes 8519680 | tf_op jit(solution)/shard_map/dot_general | solution.py:94
  75.8 1.4 dynamic-slice_bitcast_fusion.1
  77.2 5.5 %collective-permute-start.18 = (bf16[320,1280]{1,0:T(8,128)(2,1)}, bf16[320,1280]{1,0:T(8,128)(2,1)}, u32[]{:S(2)}, u32[]{:S(2)}) collective-permute-start(bf16[320,1280]{1,0:T(8,128)(2,1)} %get-tuple-element.42), channel_id=1, source_target_pairs={{0,4},{1,5},{2,6},{3,7},{16,20},{17,21},{18,22},{19,23}} | collective-permute-start | bytes 2457608 | tf_op jit(solution)/shard_map/ppermute | solution.py:113
  82.7 1.5 collective-permute-start.21
  84.2 5.4 %collective-permute-done.12 = bf16[320,1280]{1,0:T(8,128)(2,1)S(1)} collective-permute-done((bf16[320,1280]{1,0:T(8,128)(2,1)}, bf16[320,1280]{1,0:T(8,128)(2,1)S(1)}, u32[]{:S(2)}, u32[]{:S(2)}) %collective-permute-start.12) | collective-permute-done | bytes 819232 | tf_op jit(solution)/shard_map/ppermute | solution.py:67
  89.9 1.4 bitcast_dynamic-update-slice_fusion.1
  91.3 1.4 bitcast_dynamic-update-slice_fusion
  93.0 4.8 %convolution_convert_fusion.2 = bf16[1024,640]{1,0:T(8,128)(2,1)} fusion(bf16[640,1280]{1,0:T(8,128)(2,1)S(1)} %bitcast.74, bf16[256,640]{0,1:T(8,128)(2,1)S(1)} %collective-permute-done.3, bf16[256,640]{0,1:T(8,128)(2,1)S(1)} %collective-permute-done.2, bf16[256,1280]{0,1:T(8,128)(2,1)} %collective-permute-done.1, ...), kind=kOutput, calls=%fused_computation.19 | convolution fusion | flops 1691484160 | bytes 5570560 | tf_op jit(solution)/shard_map/dot_general | solution.py:122
  97.8 1.3 collective-permute-done.18
  99.1 3.5 %fusion.6 = (bf16[320,1280]{1,0:T(8,128)(2,1)}, bf16[320,1280]{1,0:T(8,128)(2,1)}) fusion(bf16[320,1280]{1,0:T(8,128)(2,1)} %collective-permute-done.18, bf16[4,320,1280]{2,1,0:T(8,128)(2,1)} %bitcast.67, s32[]{:T(128)S(6)} %min.24, s32[]{:T(128)S(6)} %min.27, bf16[320,1280]{1,0:T(8,128)(2,1)} %collective-permute-done.21), kind=kLoop, calls=%fused_computation.13 | loop fusion | flops 3276800 | bytes 4915208 | tf_op jit(solution)/shard_map/convert_element_type | solution.py:111
  102.5 5.3 %collective-permute-start.19 = (bf16[320,1280]{1,0:T(8,128)(2,1)}, bf16[320,1280]{1,0:T(8,128)(2,1)}, u32[]{:S(2)}, u32[]{:S(2)}) collective-permute-start(bf16[320,1280]{1,0:T(8,128)(2,1)} %get-tuple-element.40), channel_id=1, source_target_pairs={{0,4},{4,8},{1,5},{5,9},{2,6},{6,10},{3,7},{7,11},{16,20},{20,24},... | collective-permute-start | bytes 2457608 | tf_op jit(solution)/shard_map/ppermute | solution.py:113
  107.8 1.6 collective-permute-start.22
  109.4 4.2 %add_convert_fusion = bf16[1024,640]{1,0:T(8,128)(2,1)S(1)} fusion(bf16[1024,640]{1,0:T(8,128)(2,1)} %collective-permute-done.14, bf16[640,1280]{1,0:T(8,128)(2,1)S(1)} %bitcast.73, bf16[256,640]{0,1:T(8,128)(2,1)S(1)} %copy-done.6, bf16[256,640]{0,1:T(8,128)(2,1)S(1)} %collective-permute-done.2, bf16[256,1280]{0,1:T(8,128)(2,1)} %collective-permute-done.1, ...), kind=kOutput, calls=%fused_computation.5 | convolution fusion | flops 1694105600 | bytes 6881280 | tf_op jit(solution)/shard_map/dot_general | solution.py:122
  116.3 1.4 collective-permute-start.16
  117.9 1.6 %collective-permute-start.17 = (bf16[256,2,320]{0,2,1:T(8,128)(2,1)S(1)}, bf16[256,2,320]{0,2,1:T(8,128)(2,1)S(1)}, u32[]{:S(2)}, u32[]{:S(2)}) collective-permute-start(bf16[256,2,320]{0,2,1:T(8,128)(2,1)S(1)} %bitcast.80), channel_id=1, source_target_pairs={{0,3},{1,2},{2,1},{3,0},{4,7},{5,6},{6,5},{7,4},{8,11},{9,10},{10,... | collective-permute-start | bytes 983048 | tf_op jit(solution)/shard_map/ppermute | solution.py:12
  119.4 3.9 %collective-permute-done.19 = bf16[320,1280]{1,0:T(8,128)(2,1)} collective-permute-done((bf16[320,1280]{1,0:T(8,128)(2,1)}, bf16[320,1280]{1,0:T(8,128)(2,1)}, u32[]{:S(2)}, u32[]{:S(2)}) %collective-permute-start.19) | collective-permute-done | bytes 819232 | tf_op jit(solution)/shard_map/ppermute | solution.py:113
  123.4 3.4 %fusion.5 = (bf16[320,1280]{1,0:T(8,128)(2,1)}, bf16[320,1280]{1,0:T(8,128)(2,1)}) fusion(bf16[320,1280]{1,0:T(8,128)(2,1)} %collective-permute-done.19, bf16[4,320,1280]{2,1,0:T(8,128)(2,1)} %bitcast.68, s32[]{:T(128)S(6)} %min.25, s32[]{:T(128)S(6)} %min.28, bf16[320,1280]{1,0:T(8,128)(2,1)} %collective-permute-done.22), kind=kLoop, calls=%fused_computation.11 | loop fusion | flops 3276800 | bytes 4915208 | tf_op jit(solution)/shard_map/convert_element_type | solution.py:111
  126.8 7.2 %collective-permute-start.20 = (bf16[320,1280]{1,0:T(8,128)(2,1)}, bf16[320,1280]{1,0:T(8,128)(2,1)}, u32[]{:S(2)}, u32[]{:S(2)}) collective-permute-start(bf16[320,1280]{1,0:T(8,128)(2,1)} %get-tuple-element.38), channel_id=1, source_target_pairs={{0,4},{4,8},{8,12},{1,5},{5,9},{9,13},{2,6},{6,10},{10,14},{3,7},{... | collective-permute-start | bytes 2457608 | tf_op jit(solution)/shard_map/ppermute | solution.py:113
  134.0 1.3 collective-permute-start.23
  135.5 1.0 bitcast_dynamic-update-slice_fusion.6
  136.5 1.0 bitcast_dynamic-update-slice_fusion.5
  137.5 1.6 %copy.36 = bf16[256,2560]{1,0:T(8,128)(2,1)} copy(bf16[256,2560]{0,1:T(8,128)(2,1)S(1)} %bitcast.71) | data formatting | bytes 2621440
  139.1 9.3 %collective-permute-done.20 = bf16[320,1280]{1,0:T(8,128)(2,1)} collective-permute-done((bf16[320,1280]{1,0:T(8,128)(2,1)}, bf16[320,1280]{1,0:T(8,128)(2,1)}, u32[]{:S(2)}, u32[]{:S(2)}) %collective-permute-start.20) | collective-permute-done | bytes 819232 | tf_op jit(solution)/shard_map/ppermute | solution.py:113
  148.4 5.0 %collective-permute-done.23 = bf16[320,1280]{1,0:T(8,128)(2,1)} collective-permute-done((bf16[320,1280]{1,0:T(8,128)(2,1)}, bf16[320,1280]{1,0:T(8,128)(2,1)}, u32[]{:S(2)}, u32[]{:S(2)}) %collective-permute-start.23) | collective-permute-done | bytes 819232 | tf_op jit(solution)/shard_map/ppermute | solution.py:114
  153.5 2.9 %fusion.9 = bf16[320,1280]{1,0:T(8,128)(2,1)} fusion(bf16[320,1280]{1,0:T(8,128)(2,1)} %collective-permute-done.23, bf16[320,1280]{1,0:T(8,128)(2,1)} %collective-permute-done.20, bf16[4,320,1280]{2,1,0:T(8,128)(2,1)} %bitcast.69, s32[]{:T(128)S(6)} %min.22), kind=kLoop, calls=%fused_computation.17 | loop fusion | flops 2867200 | bytes 3276804 | tf_op jit(solution)/shard_map/convert_element_type | solution.py:118
  (51 shorter events, 7.6 us)
Async XLA Ops:
  0.6 2.3 %copy-start = (bf16[1,10,256,256]{3,2,1,0:T(8,128)(2,1)S(1)}, bf16[1,10,256,256]{3,2,1,0:T(8,128)(2,1)}, u32[]{:S(2)}) copy-start(bf16[1,10,256,256]{3,2,1,0:T(8,128)(2,1)} %param.6) | copy-start | bytes 3932164
  0.6 8.0 %copy-start.2 = (bf16[320,1280]{1,0:T(8,128)(2,1)S(1)}, bf16[320,1280]{1,0:T(8,128)(2,1)}, u32[]{:S(2)}) copy-start(bf16[320,1280]{1,0:T(8,128)(2,1)} %param.9) | copy-start | bytes 2457604
  4.1 18.0 %collective-permute-start = (bf16[256,1280]{0,1:T(8,128)(2,1)}, bf16[256,1280]{0,1:T(8,128)(2,1)}, u32[]{:S(2)}, u32[]{:S(2)}) collective-permute-start(bf16[256,1280]{0,1:T(8,128)(2,1)} %bitcast.5), channel_id=1, source_target_pairs={{0,1},{1,0},{2,3},{3,2},{4,5},{5,4},{6,7},{7,6},{8,9},{9,8},{10,11... | collective-permute-start | bytes 1966088 | tf_op jit(solution)/shard_map/ppermute | solution.py:12
  7.1 16.5 %collective-permute-start.1 = (bf16[256,1280]{0,1:T(8,128)(2,1)}, bf16[256,1280]{0,1:T(8,128)(2,1)}, u32[]{:S(2)}, u32[]{:S(2)}) collective-permute-start(bf16[256,1280]{0,1:T(8,128)(2,1)} %bitcast.5), channel_id=1, source_target_pairs={{0,2},{1,3},{2,0},{3,1},{4,6},{5,7},{6,4},{7,5},{8,10},{9,11},{10,... | collective-permute-start | bytes 1966088 | tf_op jit(solution)/shard_map/ppermute | solution.py:12
  8.6 20.4 %collective-permute-start.4 = (bf16[320,1280]{1,0:T(8,128)(2,1)S(1)}, bf16[320,1280]{1,0:T(8,128)(2,1)S(1)}, u32[]{:S(2)}, u32[]{:S(2)}) collective-permute-start(bf16[320,1280]{1,0:T(8,128)(2,1)S(1)} %copy-done.2), channel_id=1, source_target_pairs={{0,4},{4,8},{8,12},{1,5},{5,9},{9,13},{2,6},{6,10},{10,14},{3,7},{... | collective-permute-start | bytes 2457608 | tf_op jit(solution)/shard_map/ppermute | solution.py:66
  12.2 21.1 %collective-permute-start.5 = (bf16[320,1280]{1,0:T(8,128)(2,1)S(1)}, bf16[320,1280]{1,0:T(8,128)(2,1)}, u32[]{:S(2)}, u32[]{:S(2)}) collective-permute-start(bf16[320,1280]{1,0:T(8,128)(2,1)S(1)} %copy-done.2), channel_id=1, source_target_pairs={{4,0},{8,4},{12,8},{5,1},{9,5},{13,9},{6,2},{10,6},{14,10},{7,3},{... | collective-permute-start | bytes 2457608 | tf_op jit(solution)/shard_map/ppermute | solution.py:67
  23.6 11.5 %collective-permute-start.10 = (bf16[256,640]{0,1:T(8,128)(2,1)S(1)}, bf16[256,640]{0,1:T(8,128)(2,1)S(1)}, u32[]{:S(2)}, u32[]{:S(2)}) collective-permute-start(bf16[256,640]{0,1:T(8,128)(2,1)S(1)} %bitcast.79), channel_id=1, source_target_pairs={{0,3},{1,2},{2,1},{3,0},{4,7},{5,6},{6,5},{7,4},{8,11},{9,10},{10,... | collective-permute-start | bytes 983048 | tf_op jit(solution)/shard_map/ppermute | solution.py:12
  25.1 14.8 %collective-permute-start.8 = (bf16[256,640]{0,1:T(8,128)(2,1)S(1)}, bf16[256,640]{0,1:T(8,128)(2,1)S(1)}, u32[]{:S(2)}, u32[]{:S(2)}) collective-permute-start(bf16[256,640]{0,1:T(8,128)(2,1)S(1)} %bitcast.78), channel_id=1, source_target_pairs={{0,1},{1,0},{2,3},{3,2},{4,5},{5,4},{6,7},{7,6},{8,9},{9,8},{10,11... | collective-permute-start | bytes 983048 | tf_op jit(solution)/shard_map/ppermute | solution.py:12
  26.6 13.4 %collective-permute-start.9 = (bf16[256,640]{0,1:T(8,128)(2,1)S(1)}, bf16[256,640]{0,1:T(8,128)(2,1)S(1)}, u32[]{:S(2)}, u32[]{:S(2)}) collective-permute-start(bf16[256,640]{0,1:T(8,128)(2,1)S(1)} %bitcast.77), channel_id=1, source_target_pairs={{0,2},{1,3},{2,0},{3,1},{4,6},{5,7},{6,4},{7,5},{8,10},{9,11},{10,... | collective-permute-start | bytes 983048 | tf_op jit(solution)/shard_map/ppermute | solution.py:12
  29.0 10.9 %copy-start.3 = (bf16[320,1280]{1,0:T(8,128)(2,1)}, bf16[320,1280]{1,0:T(8,128)(2,1)S(1)}, u32[]{:S(2)}) copy-start(bf16[320,1280]{1,0:T(8,128)(2,1)S(1)} %collective-permute-done.4) | copy-start | bytes 2457604
  40.1 28.9 %collective-permute-start.13 = (bf16[1024,640]{0,1:T(8,128)(2,1)S(1)}, bf16[1024,640]{0,1:T(8,128)(2,1)}, u32[]{:S(2)}, u32[]{:S(2)}) collective-permute-start(bf16[1024,640]{0,1:T(8,128)(2,1)S(1)} %constant_dynamic-update-slice_fusion), channel_id=1, source_target_pairs={{0,16},{16,0},{1,17},{17,1},{2,18},{18,2},{3,19},{19,3},{4,20},{20... | collective-permute-start | bytes 3932168 | tf_op jit(solution)/shard_map/ppermute | solution.py:82
  40.2 7.4 %collective-permute-start.6 = (bf16[320,1280]{1,0:T(8,128)(2,1)}, bf16[320,1280]{1,0:T(8,128)(2,1)}, u32[]{:S(2)}, u32[]{:S(2)}) collective-permute-start(bf16[320,1280]{1,0:T(8,128)(2,1)} %copy-done.3), channel_id=1, source_target_pairs={{4,8},{8,12},{5,9},{9,13},{6,10},{10,14},{7,11},{11,15},{20,24},{2... | collective-permute-start | bytes 2457608 | tf_op jit(solution)/shard_map/ppermute | solution.py:66
  41.8 25.2 %collective-permute-start.7 = (bf16[320,1280]{1,0:T(8,128)(2,1)}, bf16[320,1280]{1,0:T(8,128)(2,1)}, u32[]{:S(2)}, u32[]{:S(2)}) collective-permute-start(bf16[320,1280]{1,0:T(8,128)(2,1)} %collective-permute-done.5), channel_id=1, source_target_pairs={{4,0},{8,4},{5,1},{9,5},{6,2},{10,6},{7,3},{11,7},{20,16},{24,20},... | collective-permute-start | bytes 2457608 | tf_op jit(solution)/shard_map/ppermute | solution.py:67
  44.5 26.0 %collective-permute-start.2 = (bf16[256,640]{0,1:T(8,128)(2,1)S(1)}, bf16[256,640]{0,1:T(8,128)(2,1)S(1)}, u32[]{:S(2)}, u32[]{:S(2)}) collective-permute-start(bf16[256,640]{0,1:T(8,128)(2,1)S(1)} %slice.28), channel_id=1, source_target_pairs={{0,2},{1,3},{2,0},{3,1},{4,6},{5,7},{6,4},{7,5},{8,10},{9,11},{10,... | collective-permute-start | bytes 983048 | tf_op jit(solution)/shard_map/ppermute | solution.py:12
  47.0 23.6 %collective-permute-start.3 = (bf16[256,640]{0,1:T(8,128)(2,1)S(1)}, bf16[256,640]{0,1:T(8,128)(2,1)S(1)}, u32[]{:S(2)}, u32[]{:S(2)}) collective-permute-start(bf16[256,640]{0,1:T(8,128)(2,1)S(1)} %slice.29), channel_id=1, source_target_pairs={{0,1},{1,0},{2,3},{3,2},{4,5},{5,4},{6,7},{7,6},{8,9},{9,8},{10,11... | collective-permute-start | bytes 983048 | tf_op jit(solution)/shard_map/ppermute | solution.py:12
  67.0 17.2 %collective-permute-start.11 = (bf16[320,1280]{1,0:T(8,128)(2,1)}, bf16[320,1280]{1,0:T(8,128)(2,1)S(1)}, u32[]{:S(2)}, u32[]{:S(2)}) collective-permute-start(bf16[320,1280]{1,0:T(8,128)(2,1)} %collective-permute-done.6), channel_id=1, source_target_pairs={{8,12},{9,13},{10,14},{11,15},{24,28},{25,29},{26,30},{27,31}} | collective-permute-start | bytes 2457608 | tf_op jit(solution)/shard_map/ppermute | solution.py:66
  67.7 21.9 %collective-permute-start.12 = (bf16[320,1280]{1,0:T(8,128)(2,1)}, bf16[320,1280]{1,0:T(8,128)(2,1)S(1)}, u32[]{:S(2)}, u32[]{:S(2)}) collective-permute-start(bf16[320,1280]{1,0:T(8,128)(2,1)} %collective-permute-done.7), channel_id=1, source_target_pairs={{4,0},{5,1},{6,2},{7,3},{20,16},{21,17},{22,18},{23,19}} | collective-permute-start | bytes 2457608 | tf_op jit(solution)/shard_map/ppermute | solution.py:67
  70.6 22.4 %copy-start.5 = (bf16[256,640]{0,1:T(8,128)(2,1)}, bf16[256,640]{0,1:T(8,128)(2,1)S(1)}, u32[]{:S(2)}) copy-start(bf16[256,640]{0,1:T(8,128)(2,1)S(1)} %collective-permute-done.3) | copy-start | bytes 983044
  75.8 14.1 %copy-start.1 = (bf16[1280,1280]{1,0:T(8,128)(2,1)}, bf16[1280,1280]{1,0:T(8,128)(2,1)S(1)}, u32[]{:S(2)}) copy-start(bf16[1280,1280]{1,0:T(8,128)(2,1)S(1)} %convolution_convert_fusion) | copy-start | bytes 9830404
  75.8 13.8 %copy-start.4 = (bf16[320,1280]{1,0:T(8,128)(2,1)S(1)}, bf16[320,1280]{1,0:T(8,128)(2,1)}, u32[]{:S(2)}) copy-start(bf16[320,1280]{1,0:T(8,128)(2,1)} %copy-done.3) | copy-start | bytes 2457604
  77.2 21.9 %collective-permute-start.18 = (bf16[320,1280]{1,0:T(8,128)(2,1)}, bf16[320,1280]{1,0:T(8,128)(2,1)}, u32[]{:S(2)}, u32[]{:S(2)}) collective-permute-start(bf16[320,1280]{1,0:T(8,128)(2,1)} %get-tuple-element.42), channel_id=1, source_target_pairs={{0,4},{1,5},{2,6},{3,7},{16,20},{17,21},{18,22},{19,23}} | collective-permute-start | bytes 2457608 | tf_op jit(solution)/shard_map/ppermute | solution.py:113
  82.7 16.4 %collective-permute-start.21 = (bf16[320,1280]{1,0:T(8,128)(2,1)}, bf16[320,1280]{1,0:T(8,128)(2,1)}, u32[]{:S(2)}, u32[]{:S(2)}) collective-permute-start(bf16[320,1280]{1,0:T(8,128)(2,1)} %get-tuple-element.43), channel_id=1, source_target_pairs={{12,8},{13,9},{14,10},{15,11},{28,24},{29,25},{30,26},{31,27}} | collective-permute-start | bytes 2457608 | tf_op jit(solution)/shard_map/ppermute | solution.py:114
  97.8 11.6 %collective-permute-start.14 = (bf16[1024,640]{1,0:T(8,128)(2,1)}, bf16[1024,640]{1,0:T(8,128)(2,1)}, u32[]{:S(2)}, u32[]{:S(2)}) collective-permute-start(bf16[1024,640]{1,0:T(8,128)(2,1)} %convolution_convert_fusion.2), channel_id=1, source_target_pairs={{0,16},{16,0},{1,17},{17,1},{2,18},{18,2},{3,19},{19,3},{4,20},{20... | collective-permute-start | bytes 3932168 | tf_op jit(solution)/shard_map/ppermute | solution.py:133
  97.8 11.6 %copy-start.6 = (bf16[256,640]{0,1:T(8,128)(2,1)S(1)}, bf16[256,640]{0,1:T(8,128)(2,1)}, u32[]{:S(2)}) copy-start(bf16[256,640]{0,1:T(8,128)(2,1)} %copy-done.5) | copy-start | bytes 983044
  102.5 20.8 %collective-permute-start.19 = (bf16[320,1280]{1,0:T(8,128)(2,1)}, bf16[320,1280]{1,0:T(8,128)(2,1)}, u32[]{:S(2)}, u32[]{:S(2)}) collective-permute-start(bf16[320,1280]{1,0:T(8,128)(2,1)} %get-tuple-element.40), channel_id=1, source_target_pairs={{0,4},{4,8},{1,5},{5,9},{2,6},{6,10},{3,7},{7,11},{16,20},{20,24},... | collective-permute-start | bytes 2457608 | tf_op jit(solution)/shard_map/ppermute | solution.py:113
  107.8 15.5 %collective-permute-start.22 = (bf16[320,1280]{1,0:T(8,128)(2,1)}, bf16[320,1280]{1,0:T(8,128)(2,1)}, u32[]{:S(2)}, u32[]{:S(2)}) collective-permute-start(bf16[320,1280]{1,0:T(8,128)(2,1)} %get-tuple-element.41), channel_id=1, source_target_pairs={{8,4},{12,8},{9,5},{13,9},{10,6},{14,10},{11,7},{15,11},{24,20},{2... | collective-permute-start | bytes 2457608 | tf_op jit(solution)/shard_map/ppermute | solution.py:114
  114.8 20.7 %collective-permute-start.15 = (bf16[256,2,320]{0,2,1:T(8,128)(2,1)}, bf16[256,2,320]{0,2,1:T(8,128)(2,1)}, u32[]{:S(2)}, u32[]{:S(2)}) collective-permute-start(bf16[256,2,320]{0,2,1:T(8,128)(2,1)} %bitcast.20), channel_id=1, source_target_pairs={{0,1},{1,0},{2,3},{3,2},{4,5},{5,4},{6,7},{7,6},{8,9},{9,8},{10,11... | collective-permute-start | bytes 983048 | tf_op jit(solution)/shard_map/ppermute | solution.py:12
  116.3 20.2 %collective-permute-start.16 = (bf16[256,2,320]{0,2,1:T(8,128)(2,1)}, bf16[256,2,320]{0,2,1:T(8,128)(2,1)}, u32[]{:S(2)}, u32[]{:S(2)}) collective-permute-start(bf16[256,2,320]{0,2,1:T(8,128)(2,1)} %bitcast.23), channel_id=1, source_target_pairs={{0,2},{1,3},{2,0},{3,1},{4,6},{5,7},{6,4},{7,5},{8,10},{9,11},{10,... | collective-permute-start | bytes 983048 | tf_op jit(solution)/shard_map/ppermute | solution.py:12
  117.9 19.7 %collective-permute-start.17 = (bf16[256,2,320]{0,2,1:T(8,128)(2,1)S(1)}, bf16[256,2,320]{0,2,1:T(8,128)(2,1)S(1)}, u32[]{:S(2)}, u32[]{:S(2)}) collective-permute-start(bf16[256,2,320]{0,2,1:T(8,128)(2,1)S(1)} %bitcast.80), channel_id=1, source_target_pairs={{0,3},{1,2},{2,1},{3,0},{4,7},{5,6},{6,5},{7,4},{8,11},{9,10},{10,... | collective-permute-start | bytes 983048 | tf_op jit(solution)/shard_map/ppermute | solution.py:12
  126.8 21.6 %collective-permute-start.20 = (bf16[320,1280]{1,0:T(8,128)(2,1)}, bf16[320,1280]{1,0:T(8,128)(2,1)}, u32[]{:S(2)}, u32[]{:S(2)}) collective-permute-start(bf16[320,1280]{1,0:T(8,128)(2,1)} %get-tuple-element.38), channel_id=1, source_target_pairs={{0,4},{4,8},{8,12},{1,5},{5,9},{9,13},{2,6},{6,10},{10,14},{3,7},{... | collective-permute-start | bytes 2457608 | tf_op jit(solution)/shard_map/ppermute | solution.py:113
  134.0 19.4 %collective-permute-start.23 = (bf16[320,1280]{1,0:T(8,128)(2,1)}, bf16[320,1280]{1,0:T(8,128)(2,1)}, u32[]{:S(2)}, u32[]{:S(2)}) collective-permute-start(bf16[320,1280]{1,0:T(8,128)(2,1)} %get-tuple-element.39), channel_id=1, source_target_pairs={{4,0},{8,4},{12,8},{5,1},{9,5},{13,9},{6,2},{10,6},{14,10},{7,3},{... | collective-permute-start | bytes 2457608 | tf_op jit(solution)/shard_map/ppermute | solution.py:114

commit v3 on v2

--- a/solution.py
+++ b/solution.py
@@ -80,9 +80,6 @@
     shares = [f_mine]
     for _ in range(1, nt):
         shares.append(lax.ppermute(shares[-1], "tensor", ring))
-    ups[2], downs[2], _ = lax.optimization_barrier((ups[2], downs[2], shares[0]))
-    for hop in range(3, no):
-        hop_on(hop)
     pieces = []
     for t in range(nt):
         piece = shares[0]
@@ -95,27 +92,34 @@
         f_all, v_all, (((0,), (0,)), ((), ())), preferred_element_type=f32
     ).astype(bf16).reshape(no, rows, width)
 
-    ups[-1], downs[-1], _ = lax.optimization_barrier((ups[-1], downs[-1], term))
+    ups[2], downs[2], _ = lax.optimization_barrier((ups[2], downs[2], term))
+    for hop in range(3, no):
+        hop_on(hop)
     w_all = jnp.zeros((no, rows, width), bf16)
     for hop in range(no):
         block = w_value if hop == 0 else jnp.where(place >= hop, ups[hop], downs[no - hop])
         w_all = lax.dynamic_update_slice(w_all, block[None], ((place - hop) % no, 0, 0))
 
-    def block_of(o):
-        return lax.dynamic_index_in_dim(term, jnp.clip(o, 0, no - 1), 0, keepdims=False)
+    def reduced(left_edge, columns):
+        def block_of(o):
+            at = (jnp.clip(o, 0, no - 1), 0, left_edge)
+            return lax.dynamic_slice(term, at, (1, rows, columns)).reshape(rows, columns)
 
-    up, down = None, None
-    for step in range(no - 1):
-        add_up, add_down = block_of(place + no - 1 - step), block_of(place - no + 1 + step)
-        if step:
-            add_up = (up.astype(f32) + add_up.astype(f32)).astype(bf16)
-            add_down = (down.astype(f32) + add_down.astype(f32)).astype(bf16)
-        up = lax.ppermute(add_up, "outer", [(k, k + 1) for k in range(min(step + 1, no - 1))])
-        down = lax.ppermute(
-            add_down, "outer", [(k, k - 1) for k in range(max(1, no - 1 - step), no)]
-        )
-    summed = block_of(place).astype(f32) + up.astype(f32) + down.astype(f32)
-    grad_weight = (summed / (no * ni)).astype(bf16)
+        up, down = None, None
+        for step in range(no - 1):
+            add_up, add_down = block_of(place + no - 1 - step), block_of(place - no + 1 + step)
+            if step:
+                add_up = (up.astype(f32) + add_up.astype(f32)).astype(bf16)
+                add_down = (down.astype(f32) + add_down.astype(f32)).astype(bf16)
+            right = [(k, k + 1) for k in range(min(step + 1, no - 1))]
+            left = [(k, k - 1) for k in range(max(1, no - 1 - step), no)]
+            up = lax.ppermute(add_up, "outer", right)
+            down = lax.ppermute(add_down, "outer", left)
+        summed = block_of(place).astype(f32) + up.astype(f32) + down.astype(f32)
+        return (summed / (no * ni)).astype(bf16)
+
+    middle = width // 512 * 256 if width >= 1024 else width // 2
+    grad_weight = jnp.concatenate([reduced(0, middle), reduced(middle, width - middle)], axis=1)
 
     def share_of(t):
         w_share = lax.dynamic_slice(w_all, (t * half, 0, 0), (half, rows, width))

time: 157 us -> 165 us (1.051)
  waiting for transfers between devices: 61.7 us -> 46.7 us
  starting transfers between devices: 45.8 us -> 55.9 us
  local copies, waits for them, and re-layouts: 17.3 us -> 24 us
  other arithmetic: 15.1 us -> 20.9 us
    ppermute x3, waiting for transfers between devices: 29.1 us -> 8.02 us  [hop_on(): downs.append(lax.ppermute(downs[-1], 'outer', left))]
    ppermute x10, waiting for transfers between devices: 11 us -> 25.8 us  [shifted(): return lax.ppermute(x, axis, pairs)]
    ppermute x6 -> x12, starting transfers between devices: 22.4 us -> 31.7 us  [the longest x6 23.2 us: reduced(): up = lax.ppermute(add_up, 'outer', right)]
    ppermute x6 -> x12, waiting for transfers between devices: 19.6 us -> 10.9 us  [the longest x6 5.7 us: reduced(): down = lax.ppermute(add_down, 'outer', left)]
    convert_element_type x3 -> x6, other arithmetic: 9.76 us -> 13.2 us  [the longest x4 9.63 us: reduced(): add_up = (up.astype(f32) + add_up.astype(f32)).astype(bf16)]
    reshape x0 -> x2, local copies, waits for them, and re-layouts: none -> 1.98 us  [block_of(): lax.dynamic_slice(term, at, (1, rows, columns)).reshape(rows, columns)]
    dynamic_slice x1, local copies, waits for them, and re-layouts: 0.22 us -> 2.2 us  [share_of(): w_share = lax.dynamic_slice(w_all, (t * half, 0, 0), (half, rows, width))]
    broadcast_in_dim x1, local copies, waits for them, and re-layouts: 0.22 us -> 1.93 us  [local(): w_all = jnp.zeros((no, rows, width), bf16)]
  transfers between devices with their start and end apart: 24 -> 30, of which waited for: 12 -> 15; matrix products, arithmetic and copies ran while one was open for 26% -> 30% of each run, Pallas kernels for 0% -> 0%
where the time goes in v3:
time: 165 us; the launch traced here: 164 us
  starting transfers between devices  55.9 us (34%)
  waiting for transfers between devices  46.7 us (28%)
  local copies, waits for them, and re-layouts  24 us (15%)
  other arithmetic  20.9 us (13%)
  matrix products  15.4 us (9%)
    ppermute x10, waiting for transfers between devices, shifted(): return lax.ppermute(x, axis, pairs)  25.8 us
    ppermute x6, starting transfers between devices, reduced(): up = lax.ppermute(add_up, 'outer', right)  23.2 us
    ppermute x10, starting transfers between devices, shifted(): return lax.ppermute(x, axis, pairs)  13.6 us
    convert_element_type x4, other arithmetic, reduced(): add_up = (up.astype(f32) + add_up.astype(f32)).astype(bf16)  9.63 us
    dot_general x2, matrix products, share_of(): lax.dot_general(v_all, w_share.reshape(half * rows, width), (((1,), (1,))...  8.98 us
    ppermute x6, starting transfers between devices, reduced(): down = lax.ppermute(add_down, 'outer', left)  8.49 us
    ppermute x3, waiting for transfers between devices, hop_on(): downs.append(lax.ppermute(downs[-1], 'outer', left))  8.02 us
    ppermute x3, starting transfers between devices, hop_on(): ups.append(lax.ppermute(ups[-1], 'outer', right))  6.7 us
  transfers between devices with their start and end apart: 30, of which 15 were waited for; matrix products, arithmetic and copies ran while one was open for 30% of the time, Pallas kernels for 0%

profile of v3, /device:TPU:0, one launch (start us, length us, event | category | flops | bytes accessed | tf_op | source)
XLA Modules:
  0.0 163.9 jit_solution(13400841444828193200)
XLA Ops:
  0.7 1.5 copy.25
  4.1 3.0 %collective-permute-start = (bf16[256,1280]{0,1:T(8,128)(2,1)}, bf16[256,1280]{0,1:T(8,128)(2,1)}, u32[]{:S(2)}, u32[]{:S(2)}) collective-permute-start(bf16[256,1280]{0,1:T(8,128)(2,1)} %bitcast.5), channel_id=1, source_target_pairs={{0,1},{1,0},{2,3},{3,2},{4,5},{5,4},{6,7},{7,6},{8,9},{9,8},{10,11... | collective-permute-start | bytes 1966088 | tf_op jit(solution)/shard_map/ppermute | solution.py:12
  7.1 1.5 collective-permute-start.1
  8.6 4.4 %collective-permute-start.4 = (bf16[320,1280]{1,0:T(8,128)(2,1)S(1)}, bf16[320,1280]{1,0:T(8,128)(2,1)}, u32[]{:S(2)}, u32[]{:S(2)}) collective-permute-start(bf16[320,1280]{1,0:T(8,128)(2,1)S(1)} %copy-done.3), channel_id=1, source_target_pairs={{0,4},{4,8},{8,12},{1,5},{5,9},{9,13},{2,6},{6,10},{10,14},{3,7},{... | collective-permute-start | bytes 2457608 | tf_op jit(solution)/shard_map/ppermute | solution.py:66
  14.4 4.4 %copy.26 = bf16[256,5120]{0,1:T(8,128)(2,1)} copy(bf16[256,5120]{1,0:T(8,128)(2,1)} %param.5) | data formatting | bytes 5242880 | tf_op jit(solution)/shard_map/optimization_barrier | solution.py:39
  20.1 2.0 %collective-permute-done = bf16[256,1280]{0,1:T(8,128)(2,1)} collective-permute-done((bf16[256,1280]{0,1:T(8,128)(2,1)}, bf16[256,1280]{0,1:T(8,128)(2,1)}, u32[]{:S(2)}, u32[]{:S(2)}) %collective-permute-start) | collective-permute-done | bytes 655392 | tf_op jit(solution)/shard_map/ppermute | solution.py:12
  22.1 1.5 collective-permute-done.1
  23.6 1.5 collective-permute-start.10
  25.1 1.5 collective-permute-start.8
  27.1 1.9 %collective-permute-done.4 = bf16[320,1280]{1,0:T(8,128)(2,1)} collective-permute-done((bf16[320,1280]{1,0:T(8,128)(2,1)S(1)}, bf16[320,1280]{1,0:T(8,128)(2,1)}, u32[]{:S(2)}, u32[]{:S(2)}) %collective-permute-start.4) | collective-permute-done | bytes 819232 | tf_op jit(solution)/shard_map/ppermute | solution.py:66
  29.0 5.1 %collective-permute-done.5 = bf16[320,1280]{1,0:T(8,128)(2,1)S(1)} collective-permute-done((bf16[320,1280]{1,0:T(8,128)(2,1)S(1)}, bf16[320,1280]{1,0:T(8,128)(2,1)S(1)}, u32[]{:S(2)}, u32[]{:S(2)}) %collective-permute-start.5) | collective-permute-done | bytes 819232 | tf_op jit(solution)/shard_map/ppermute | solution.py:67
  35.1 4.8 %collective-permute-done.8 = bf16[256,640]{0,1:T(8,128)(2,1)S(1)} collective-permute-done((bf16[256,640]{0,1:T(8,128)(2,1)S(1)}, bf16[256,640]{0,1:T(8,128)(2,1)S(1)}, u32[]{:S(2)}, u32[]{:S(2)}) %collective-permute-start.8) | collective-permute-done | bytes 327712 | tf_op jit(solution)/shard_map/ppermute | solution.py:12
  41.2 1.5 collective-permute-start.2
  44.3 1.6 collective-permute-start.6
  47.2 1.5 broadcast_select_fusion.1
  48.7 2.7 %collective-permute-done.2 = bf16[256,640]{0,1:T(8,128)(2,1)S(1)} collective-permute-done((bf16[256,640]{0,1:T(8,128)(2,1)S(1)}, bf16[256,640]{0,1:T(8,128)(2,1)S(1)}, u32[]{:S(2)}, u32[]{:S(2)}) %collective-permute-start.2) | collective-permute-done | bytes 327712 | tf_op jit(solution)/shard_map/ppermute | solution.py:12
  51.4 2.2 %collective-permute-done.3 = bf16[256,640]{0,1:T(8,128)(2,1)S(1)} collective-permute-done((bf16[256,640]{0,1:T(8,128)(2,1)S(1)}, bf16[256,640]{0,1:T(8,128)(2,1)S(1)}, u32[]{:S(2)}, u32[]{:S(2)}) %collective-permute-start.3) | collective-permute-done | bytes 327712 | tf_op jit(solution)/shard_map/ppermute | solution.py:12
  53.6 5.2 %convolution_convert_fusion = bf16[1280,1280]{1,0:T(8,128)(2,1)S(1)} fusion(bf16[1024,640]{0,1:T(8,128)(2,1)S(1)} %get-tuple-element.49, bf16[1024,640]{0,1:T(8,128)(2,1)S(1)} %get-tuple-element.48, bf16[256,640]{0,1:T(8,128)(2,1)S(1)} %collective-permute-done.3, bf16[256,640]{0,1:T(8,128)(2,1)S(1)} %collective-permute-done.2, ...), kind=kOutput, calls=%fused_computation | convolution fusion | flops 3375431680 | bytes 8519680 | tf_op jit(solution)/shard_map/dot_general | solution.py:91
  59.8 4.2 %collective-permute-start.18 = (bf16[320,512]{1,0:T(8,128)(2,1)}, bf16[320,512]{1,0:T(8,128)(2,1)}, u32[]{:S(2)}, u32[]{:S(2)}) collective-permute-start(bf16[320,512]{1,0:T(8,128)(2,1)} %get-tuple-element.38), channel_id=1, source_target_pairs={{0,4},{1,5},{2,6},{3,7},{16,20},{17,21},{18,22},{19,23}} | collective-permute-start | bytes 983048 | tf_op jit(solution)/shard_map/ppermute | solution.py:116
  64.0 1.4 collective-permute-start.21
  67.7 1.5 collective-permute-start.27
  71.8 1.9 %broadcast_in_dim.30 = bf16[4,320,1280]{2,1,0:T(8,128)(2,1)} broadcast(bf16[]{:T(256)} %constant.83.clone.1), dimensions={} | broadcast | bytes 3276802 | tf_op jit(solution)/shard_map/broadcast_in_dim | solution.py:98
  75.4 2.3 %fusion.14 = (bf16[320,512]{1,0:T(8,128)(2,1)}, bf16[320,512]{1,0:T(8,128)(2,1)}) fusion(bf16[320,512]{1,0:T(8,128)(2,1)} %collective-permute-done.18, bf16[4,320,1280]{2,1,0:T(8,128)(2,1)} %bitcast.87, s32[]{:T(128)S(6)} %min.31, s32[]{:T(128)S(6)} %min.34, bf16[320,512]{1,0:T(8,128)(2,1)} %collective-permute-done.21), kind=kLoop, calls=%fused_computation.36 | loop fusion | flops 1310720 | bytes 1966088 | tf_op jit(solution)/shard_map/convert_element_type | solution.py:112
  77.7 5.4 %collective-permute-start.19 = (bf16[320,512]{1,0:T(8,128)(2,1)}, bf16[320,512]{1,0:T(8,128)(2,1)}, u32[]{:S(2)}, u32[]{:S(2)}) collective-permute-start(bf16[320,512]{1,0:T(8,128)(2,1)} %get-tuple-element.36), channel_id=1, source_target_pairs={{0,4},{4,8},{1,5},{5,9},{2,6},{6,10},{3,7},{7,11},{16,20},{20,24},... | collective-permute-start | bytes 983048 | tf_op jit(solution)/shard_map/ppermute | solution.py:116
  83.1 1.4 collective-permute-start.22
  84.5 2.5 %fusion.7 = (bf16[320,768]{1,0:T(8,128)(2,1)}, bf16[320,768]{1,0:T(8,128)(2,1)}) fusion(bf16[320,768]{1,0:T(8,128)(2,1)S(1)} %collective-permute-done.24, bf16[4,320,1280]{2,1,0:T(8,128)(2,1)} %bitcast.88, s32[]{:T(128)S(6)} %min.31, s32[]{:T(128)S(6)} %min.34, bf16[320,768]{1,0:T(8,128)(2,1)} %collective-permute-done.27), kind=kLoop, calls=%fused_computation.19 | loop fusion | flops 1966080 | bytes 2949128 | tf_op jit(solution)/shard_map/convert_element_type | solution.py:112
  87.0 3.2 %collective-permute-start.25 = (bf16[320,768]{1,0:T(8,128)(2,1)}, bf16[320,768]{1,0:T(8,128)(2,1)S(1)}, u32[]{:S(2)}, u32[]{:S(2)}) collective-permute-start(bf16[320,768]{1,0:T(8,128)(2,1)} %get-tuple-element.42), channel_id=1, source_target_pairs={{0,4},{4,8},{1,5},{5,9},{2,6},{6,10},{3,7},{7,11},{16,20},{20,24},... | collective-permute-start | bytes 1474568 | tf_op jit(solution)/shard_map/ppermute | solution.py:116
  90.2 1.6 collective-permute-done.12
  91.8 1.5 collective-permute-start.28
  94.4 2.2 %bitcast_dynamic-update-slice_fusion.1 = bf16[4,320,1280]{2,1,0:T(8,128)(2,1)} fusion(bf16[4,320,1280]{2,1,0:T(8,128)(2,1)} %bitcast_dynamic-update-slice_fusion.2, s32[]{:T(128)S(6)} %select_n.140, bf16[320,1280]{1,0:T(8,128)(2,1)} %collective-permute-done.6, bf16[320,1280]{1,0:T(8,128)(2,1)} %collective-permute-done.7, pred[]{:T(512)S(6)} %ge.10), kind=kLoop, calls=%fused_computation.26 | loop fusion | flops 409600 | bytes 2457605 | tf_op jit(solution)/shard_map/dynamic_update_slice | solution.py:101
  97.7 2.2 %constant_dynamic-slice_fusion = (bf16[2,320,1280]{2,1,0:T(8,128)(2,1)S(1)}, bf16[2,320,1280]{2,1,0:T(8,128)(2,1)S(1)}) fusion(bf16[4,320,1280]{2,1,0:T(8,128)(2,1)} %bitcast_dynamic-update-slice_fusion, s32[]{:T(128)S(6)} %select_n.148, s32[]{:T(128)S(6)} %select_n.146), kind=kLoop, calls=%fused_computation.57 | loop fusion | bytes 6553608 | tf_op jit(solution)/shard_map/dynamic_slice | solution.py:125
  100.0 4.8 %convolution_convert_fusion.2 = bf16[1024,640]{1,0:T(8,128)(2,1)} fusion(bf16[640,1280]{1,0:T(8,128)(2,1)S(1)} %bitcast.97, bf16[256,640]{0,1:T(8,128)(2,1)S(1)} %copy-done.11, bf16[256,640]{0,1:T(8,128)(2,1)S(1)} %copy-done.8, bf16[256,1280]{0,1:T(8,128)(2,1)} %collective-permute-done.1, bf16[256,1280]{0,1:T(8,128)(2,1)} %collective-permute-done, ...), kind=kOutput, calls=%fused_computation.7 | convolution fusion | flops 1691484160 | bytes 5570560 | tf_op jit(solution)/shard_map/dot_general | solution.py:126
  104.8 2.3 %fusion.13 = (bf16[320,512]{1,0:T(8,128)(2,1)}, bf16[320,512]{1,0:T(8,128)(2,1)}) fusion(bf16[320,512]{1,0:T(8,128)(2,1)} %collective-permute-done.19, bf16[4,320,1280]{2,1,0:T(8,128)(2,1)} %bitcast.89, s32[]{:T(128)S(6)} %min.32, s32[]{:T(128)S(6)} %min.35, bf16[320,512]{1,0:T(8,128)(2,1)} %collective-permute-done.22), kind=kLoop, calls=%fused_computation.34 | loop fusion | flops 1310720 | bytes 1966088 | tf_op jit(solution)/shard_map/convert_element_type | solution.py:112
  107.1 4.6 %collective-permute-start.20 = (bf16[320,512]{1,0:T(8,128)(2,1)}, bf16[320,512]{1,0:T(8,128)(2,1)}, u32[]{:S(2)}, u32[]{:S(2)}) collective-permute-start(bf16[320,512]{1,0:T(8,128)(2,1)} %get-tuple-element.34), channel_id=1, source_target_pairs={{0,4},{4,8},{8,12},{1,5},{5,9},{9,13},{2,6},{6,10},{10,14},{3,7},{... | collective-permute-start | bytes 983048 | tf_op jit(solution)/shard_map/ppermute | solution.py:116
  113.0 2.5 %fusion.6 = (bf16[320,768]{1,0:T(8,128)(2,1)}, bf16[320,768]{1,0:T(8,128)(2,1)}) fusion(bf16[320,768]{1,0:T(8,128)(2,1)S(1)} %collective-permute-done.25, bf16[4,320,1280]{2,1,0:T(8,128)(2,1)} %bitcast.90, s32[]{:T(128)S(6)} %min.32, s32[]{:T(128)S(6)} %min.35, bf16[320,768]{1,0:T(8,128)(2,1)} %collective-permute-done.28), kind=kLoop, calls=%fused_computation.17 | loop fusion | flops 1966080 | bytes 2949128 | tf_op jit(solution)/shard_map/convert_element_type | solution.py:112
  115.5 4.6 %collective-permute-start.26 = (bf16[320,768]{1,0:T(8,128)(2,1)}, bf16[320,768]{1,0:T(8,128)(2,1)S(1)}, u32[]{:S(2)}, u32[]{:S(2)}) collective-permute-start(bf16[320,768]{1,0:T(8,128)(2,1)} %get-tuple-element.40), channel_id=1, source_target_pairs={{0,4},{4,8},{8,12},{1,5},{5,9},{9,13},{2,6},{6,10},{10,14},{3,7},{... | collective-permute-start | bytes 1474568 | tf_op jit(solution)/shard_map/ppermute | solution.py:116
  120.1 1.5 collective-permute-start.29
  121.6 2.3 %collective-permute-done.23 = bf16[320,512]{1,0:T(8,128)(2,1)} collective-permute-done((bf16[320,512]{1,0:T(8,128)(2,1)}, bf16[320,512]{1,0:T(8,128)(2,1)}, u32[]{:S(2)}, u32[]{:S(2)}) %collective-permute-start.23) | collective-permute-done | bytes 327712 | tf_op jit(solution)/shard_map/ppermute | solution.py:117
  123.9 2.0 %fusion.17 = bf16[320,512]{1,0:T(8,128)(2,1)} fusion(bf16[320,512]{1,0:T(8,128)(2,1)} %collective-permute-done.23, bf16[320,512]{1,0:T(8,128)(2,1)} %collective-permute-done.20, bf16[4,320,1280]{2,1,0:T(8,128)(2,1)} %bitcast.91, s32[]{:T(128)S(6)} %min.29), kind=kLoop, calls=%fused_computation.40 | loop fusion | flops 1146880 | bytes 1310724 | tf_op jit(solution)/shard_map/convert_element_type | solution.py:119
  126.0 5.2 %collective-permute-done.26 = bf16[320,768]{1,0:T(8,128)(2,1)S(1)} collective-permute-done((bf16[320,768]{1,0:T(8,128)(2,1)}, bf16[320,768]{1,0:T(8,128)(2,1)S(1)}, u32[]{:S(2)}, u32[]{:S(2)}) %collective-permute-start.26) | collective-permute-done | bytes 491552 | tf_op jit(solution)/shard_map/ppermute | solution.py:116
  131.9 3.4 %collective-permute-done.29 = bf16[320,768]{1,0:T(8,128)(2,1)} collective-permute-done((bf16[320,768]{1,0:T(8,128)(2,1)}, bf16[320,768]{1,0:T(8,128)(2,1)}, u32[]{:S(2)}, u32[]{:S(2)}) %collective-permute-start.29) | collective-permute-done | bytes 491552 | tf_op jit(solution)/shard_map/ppermute | solution.py:117
  135.3 1.5 fusion.10
  136.8 4.2 %add_convert_fusion = bf16[1024,640]{1,0:T(8,128)(2,1)S(1)} fusion(bf16[1024,640]{1,0:T(8,128)(2,1)} %collective-permute-done.14, bf16[640,1280]{1,0:T(8,128)(2,1)S(1)} %bitcast.96, bf16[256,640]{0,1:T(8,128)(2,1)S(1)} %copy-done.12, bf16[256,640]{0,1:T(8,128)(2,1)S(1)} %copy-done.9, bf16[256,1280]{0,1:T(8,128)(2,1)} %collective-permute-done.1, ...), kind=kOutput, calls=%fused_computation.5 | convolution fusion | flops 1694105600 | bytes 6881280 | tf_op jit(solution)/shard_map/dot_general | solution.py:126
  142.1 1.5 collective-permute-start.15
  147.1 1.4 collective-permute-start.17
  148.6 4.1 %collective-permute-done.15 = bf16[256,2,320]{0,2,1:T(8,128)(2,1)} collective-permute-done((bf16[256,2,320]{0,2,1:T(8,128)(2,1)}, bf16[256,2,320]{0,2,1:T(8,128)(2,1)}, u32[]{:S(2)}, u32[]{:S(2)}) %collective-permute-start.15) | collective-permute-done | bytes 327712 | tf_op jit(solution)/shard_map/ppermute | solution.py:12
  153.7 7.5 %collective-permute-done.16 = bf16[256,2,320]{0,2,1:T(8,128)(2,1)} collective-permute-done((bf16[256,2,320]{0,2,1:T(8,128)(2,1)}, bf16[256,2,320]{0,2,1:T(8,128)(2,1)}, u32[]{:S(2)}, u32[]{:S(2)}) %collective-permute-start.16) | collective-permute-done | bytes 327712 | tf_op jit(solution)/shard_map/ppermute | solution.py:12
  162.3 1.6 copy.36
  (80 shorter events, 28.9 us)
Async XLA Ops:
  0.6 2.3 %copy-start = (bf16[1,10,256,256]{3,2,1,0:T(8,128)(2,1)S(1)}, bf16[1,10,256,256]{3,2,1,0:T(8,128)(2,1)}, u32[]{:S(2)}) copy-start(bf16[1,10,256,256]{3,2,1,0:T(8,128)(2,1)} %param.6) | copy-start | bytes 3932164
  0.6 8.0 %copy-start.3 = (bf16[320,1280]{1,0:T(8,128)(2,1)S(1)}, bf16[320,1280]{1,0:T(8,128)(2,1)}, u32[]{:S(2)}) copy-start(bf16[320,1280]{1,0:T(8,128)(2,1)} %param.9) | copy-start | bytes 2457604
  4.1 18.0 %collective-permute-start = (bf16[256,1280]{0,1:T(8,128)(2,1)}, bf16[256,1280]{0,1:T(8,128)(2,1)}, u32[]{:S(2)}, u32[]{:S(2)}) collective-permute-start(bf16[256,1280]{0,1:T(8,128)(2,1)} %bitcast.5), channel_id=1, source_target_pairs={{0,1},{1,0},{2,3},{3,2},{4,5},{5,4},{6,7},{7,6},{8,9},{9,8},{10,11... | collective-permute-start | bytes 1966088 | tf_op jit(solution)/shard_map/ppermute | solution.py:12
  7.1 16.5 %collective-permute-start.1 = (bf16[256,1280]{0,1:T(8,128)(2,1)}, bf16[256,1280]{0,1:T(8,128)(2,1)}, u32[]{:S(2)}, u32[]{:S(2)}) collective-permute-start(bf16[256,1280]{0,1:T(8,128)(2,1)} %bitcast.5), channel_id=1, source_target_pairs={{0,2},{1,3},{2,0},{3,1},{4,6},{5,7},{6,4},{7,5},{8,10},{9,11},{10,... | collective-permute-start | bytes 1966088 | tf_op jit(solution)/shard_map/ppermute | solution.py:12
  8.6 20.4 %collective-permute-start.4 = (bf16[320,1280]{1,0:T(8,128)(2,1)S(1)}, bf16[320,1280]{1,0:T(8,128)(2,1)}, u32[]{:S(2)}, u32[]{:S(2)}) collective-permute-start(bf16[320,1280]{1,0:T(8,128)(2,1)S(1)} %copy-done.3), channel_id=1, source_target_pairs={{0,4},{4,8},{8,12},{1,5},{5,9},{9,13},{2,6},{6,10},{10,14},{3,7},{... | collective-permute-start | bytes 2457608 | tf_op jit(solution)/shard_map/ppermute | solution.py:66
  13.0 21.0 %collective-permute-start.5 = (bf16[320,1280]{1,0:T(8,128)(2,1)S(1)}, bf16[320,1280]{1,0:T(8,128)(2,1)S(1)}, u32[]{:S(2)}, u32[]{:S(2)}) collective-permute-start(bf16[320,1280]{1,0:T(8,128)(2,1)S(1)} %copy-done.3), channel_id=1, source_target_pairs={{4,0},{8,4},{12,8},{5,1},{9,5},{13,9},{6,2},{10,6},{14,10},{7,3},{... | collective-permute-start | bytes 2457608 | tf_op jit(solution)/shard_map/ppermute | solution.py:67
  23.6 11.5 %collective-permute-start.10 = (bf16[256,640]{0,1:T(8,128)(2,1)S(1)}, bf16[256,640]{0,1:T(8,128)(2,1)S(1)}, u32[]{:S(2)}, u32[]{:S(2)}) collective-permute-start(bf16[256,640]{0,1:T(8,128)(2,1)S(1)} %bitcast.102), channel_id=1, source_target_pairs={{0,3},{1,2},{2,1},{3,0},{4,7},{5,6},{6,5},{7,4},{8,11},{9,10},{10,... | collective-permute-start | bytes 983048 | tf_op jit(solution)/shard_map/ppermute | solution.py:12
  25.1 14.8 %collective-permute-start.8 = (bf16[256,640]{0,1:T(8,128)(2,1)S(1)}, bf16[256,640]{0,1:T(8,128)(2,1)S(1)}, u32[]{:S(2)}, u32[]{:S(2)}) collective-permute-start(bf16[256,640]{0,1:T(8,128)(2,1)S(1)} %bitcast.101), channel_id=1, source_target_pairs={{0,1},{1,0},{2,3},{3,2},{4,5},{5,4},{6,7},{7,6},{8,9},{9,8},{10,11... | collective-permute-start | bytes 983048 | tf_op jit(solution)/shard_map/ppermute | solution.py:12
  26.6 13.4 %collective-permute-start.9 = (bf16[256,640]{0,1:T(8,128)(2,1)S(1)}, bf16[256,640]{0,1:T(8,128)(2,1)S(1)}, u32[]{:S(2)}, u32[]{:S(2)}) collective-permute-start(bf16[256,640]{0,1:T(8,128)(2,1)S(1)} %bitcast.100), channel_id=1, source_target_pairs={{0,2},{1,3},{2,0},{3,1},{4,6},{5,7},{6,4},{7,5},{8,10},{9,11},{10,... | collective-permute-start | bytes 983048 | tf_op jit(solution)/shard_map/ppermute | solution.py:12
  34.1 5.9 %copy-start.4 = (bf16[320,1280]{1,0:T(8,128)(2,1)}, bf16[320,1280]{1,0:T(8,128)(2,1)S(1)}, u32[]{:S(2)}) copy-start(bf16[320,1280]{1,0:T(8,128)(2,1)S(1)} %collective-permute-done.5) | copy-start | bytes 2457604
  40.1 7.1 %collective-permute-start.11 = (bf16[1024,640]{0,1:T(8,128)(2,1)S(1)}, bf16[1024,640]{0,1:T(8,128)(2,1)}, u32[]{:S(2)}, u32[]{:S(2)}) collective-permute-start(bf16[1024,640]{0,1:T(8,128)(2,1)S(1)} %constant_dynamic-update-slice_fusion), channel_id=1, source_target_pairs={{0,16},{16,0},{1,17},{17,1},{2,18},{18,2},{3,19},{19,3},{4,20},{20... | collective-permute-start | bytes 3932168 | tf_op jit(solution)/shard_map/ppermute | solution.py:82
  41.2 10.1 %collective-permute-start.2 = (bf16[256,640]{0,1:T(8,128)(2,1)S(1)}, bf16[256,640]{0,1:T(8,128)(2,1)S(1)}, u32[]{:S(2)}, u32[]{:S(2)}) collective-permute-start(bf16[256,640]{0,1:T(8,128)(2,1)S(1)} %slice.28), channel_id=1, source_target_pairs={{0,2},{1,3},{2,0},{3,1},{4,6},{5,7},{6,4},{7,5},{8,10},{9,11},{10,... | collective-permute-start | bytes 983048 | tf_op jit(solution)/shard_map/ppermute | solution.py:12
  43.7 9.8 %collective-permute-start.3 = (bf16[256,640]{0,1:T(8,128)(2,1)S(1)}, bf16[256,640]{0,1:T(8,128)(2,1)S(1)}, u32[]{:S(2)}, u32[]{:S(2)}) collective-permute-start(bf16[256,640]{0,1:T(8,128)(2,1)S(1)} %slice.29), channel_id=1, source_target_pairs={{0,1},{1,0},{2,3},{3,2},{4,5},{5,4},{6,7},{7,6},{8,9},{9,8},{10,11... | collective-permute-start | bytes 983048 | tf_op jit(solution)/shard_map/ppermute | solution.py:12
  44.3 23.4 %collective-permute-start.6 = (bf16[320,1280]{1,0:T(8,128)(2,1)}, bf16[320,1280]{1,0:T(8,128)(2,1)}, u32[]{:S(2)}, u32[]{:S(2)}) collective-permute-start(bf16[320,1280]{1,0:T(8,128)(2,1)} %collective-permute-done.4), channel_id=1, source_target_pairs={{4,8},{8,12},{5,9},{9,13},{6,10},{10,14},{7,11},{11,15},{20,24},{2... | collective-permute-start | bytes 2457608 | tf_op jit(solution)/shard_map/ppermute | solution.py:66
  45.9 24.6 %collective-permute-start.7 = (bf16[320,1280]{1,0:T(8,128)(2,1)}, bf16[320,1280]{1,0:T(8,128)(2,1)}, u32[]{:S(2)}, u32[]{:S(2)}) collective-permute-start(bf16[320,1280]{1,0:T(8,128)(2,1)} %copy-done.4), channel_id=1, source_target_pairs={{4,0},{8,4},{5,1},{9,5},{6,2},{10,6},{7,3},{11,7},{20,16},{24,20},... | collective-permute-start | bytes 2457608 | tf_op jit(solution)/shard_map/ppermute | solution.py:67
  51.4 7.4 %copy-start.7 = (bf16[256,640]{0,1:T(8,128)(2,1)}, bf16[256,640]{0,1:T(8,128)(2,1)S(1)}, u32[]{:S(2)}) copy-start(bf16[256,640]{0,1:T(8,128)(2,1)S(1)} %collective-permute-done.2) | copy-start | bytes 983044
  53.6 5.2 %copy-start.10 = (bf16[256,640]{0,1:T(8,128)(2,1)}, bf16[256,640]{0,1:T(8,128)(2,1)S(1)}, u32[]{:S(2)}) copy-start(bf16[256,640]{0,1:T(8,128)(2,1)S(1)} %collective-permute-done.3) | copy-start | bytes 983044
  58.8 15.0 %copy-start.1 = (bf16[1280,1280]{1,0:T(8,128)(2,1)}, bf16[1280,1280]{1,0:T(8,128)(2,1)S(1)}, u32[]{:S(2)}) copy-start(bf16[1280,1280]{1,0:T(8,128)(2,1)S(1)} %convolution_convert_fusion) | copy-start | bytes 9830404
  59.8 14.9 %collective-permute-start.18 = (bf16[320,512]{1,0:T(8,128)(2,1)}, bf16[320,512]{1,0:T(8,128)(2,1)}, u32[]{:S(2)}, u32[]{:S(2)}) collective-permute-start(bf16[320,512]{1,0:T(8,128)(2,1)} %get-tuple-element.38), channel_id=1, source_target_pairs={{0,4},{1,5},{2,6},{3,7},{16,20},{17,21},{18,22},{19,23}} | collective-permute-start | bytes 983048 | tf_op jit(solution)/shard_map/ppermute | solution.py:116
  64.0 11.4 %collective-permute-start.21 = (bf16[320,512]{1,0:T(8,128)(2,1)}, bf16[320,512]{1,0:T(8,128)(2,1)}, u32[]{:S(2)}, u32[]{:S(2)}) collective-permute-start(bf16[320,512]{1,0:T(8,128)(2,1)} %get-tuple-element.39), channel_id=1, source_target_pairs={{12,8},{13,9},{14,10},{15,11},{28,24},{29,25},{30,26},{31,27}} | collective-permute-start | bytes 983048 | tf_op jit(solution)/shard_map/ppermute | solution.py:117
  66.4 16.7 %collective-permute-start.24 = (bf16[320,768]{1,0:T(8,128)(2,1)}, bf16[320,768]{1,0:T(8,128)(2,1)S(1)}, u32[]{:S(2)}, u32[]{:S(2)}) collective-permute-start(bf16[320,768]{1,0:T(8,128)(2,1)} %get-tuple-element.44), channel_id=1, source_target_pairs={{0,4},{1,5},{2,6},{3,7},{16,20},{17,21},{18,22},{19,23}} | collective-permute-start | bytes 1474568 | tf_op jit(solution)/shard_map/ppermute | solution.py:116
  67.7 16.8 %collective-permute-start.27 = (bf16[320,768]{1,0:T(8,128)(2,1)}, bf16[320,768]{1,0:T(8,128)(2,1)}, u32[]{:S(2)}, u32[]{:S(2)}) collective-permute-start(bf16[320,768]{1,0:T(8,128)(2,1)} %get-tuple-element.45), channel_id=1, source_target_pairs={{12,8},{13,9},{14,10},{15,11},{28,24},{29,25},{30,26},{31,27}} | collective-permute-start | bytes 1474568 | tf_op jit(solution)/shard_map/ppermute | solution.py:117
  70.5 21.3 %collective-permute-start.12 = (bf16[320,1280]{1,0:T(8,128)(2,1)}, bf16[320,1280]{1,0:T(8,128)(2,1)S(1)}, u32[]{:S(2)}, u32[]{:S(2)}) collective-permute-start(bf16[320,1280]{1,0:T(8,128)(2,1)} %collective-permute-done.7), channel_id=1, source_target_pairs={{4,0},{5,1},{6,2},{7,3},{20,16},{21,17},{22,18},{23,19}} | collective-permute-start | bytes 2457608 | tf_op jit(solution)/shard_map/ppermute | solution.py:67
  74.7 21.9 %collective-permute-start.13 = (bf16[320,1280]{1,0:T(8,128)(2,1)}, bf16[320,1280]{1,0:T(8,128)(2,1)S(1)}, u32[]{:S(2)}, u32[]{:S(2)}) collective-permute-start(bf16[320,1280]{1,0:T(8,128)(2,1)} %collective-permute-done.6), channel_id=1, source_target_pairs={{8,12},{9,13},{10,14},{11,15},{24,28},{25,29},{26,30},{27,31}} | collective-permute-start | bytes 2457608 | tf_op jit(solution)/shard_map/ppermute | solution.py:66
  77.7 27.1 %collective-permute-start.19 = (bf16[320,512]{1,0:T(8,128)(2,1)}, bf16[320,512]{1,0:T(8,128)(2,1)}, u32[]{:S(2)}, u32[]{:S(2)}) collective-permute-start(bf16[320,512]{1,0:T(8,128)(2,1)} %get-tuple-element.36), channel_id=1, source_target_pairs={{0,4},{4,8},{1,5},{5,9},{2,6},{6,10},{3,7},{7,11},{16,20},{20,24},... | collective-permute-start | bytes 983048 | tf_op jit(solution)/shard_map/ppermute | solution.py:116
  83.1 21.7 %collective-permute-start.22 = (bf16[320,512]{1,0:T(8,128)(2,1)}, bf16[320,512]{1,0:T(8,128)(2,1)}, u32[]{:S(2)}, u32[]{:S(2)}) collective-permute-start(bf16[320,512]{1,0:T(8,128)(2,1)} %get-tuple-element.37), channel_id=1, source_target_pairs={{8,4},{12,8},{9,5},{13,9},{10,6},{14,10},{11,7},{15,11},{24,20},{2... | collective-permute-start | bytes 983048 | tf_op jit(solution)/shard_map/ppermute | solution.py:117
  87.0 9.6 %copy-start.5 = (bf16[320,1280]{1,0:T(8,128)(2,1)S(1)}, bf16[320,1280]{1,0:T(8,128)(2,1)}, u32[]{:S(2)}) copy-start(bf16[320,1280]{1,0:T(8,128)(2,1)} %copy-done.4) | copy-start | bytes 2457604
  87.0 25.9 %collective-permute-start.25 = (bf16[320,768]{1,0:T(8,128)(2,1)}, bf16[320,768]{1,0:T(8,128)(2,1)S(1)}, u32[]{:S(2)}, u32[]{:S(2)}) collective-permute-start(bf16[320,768]{1,0:T(8,128)(2,1)} %get-tuple-element.42), channel_id=1, source_target_pairs={{0,4},{4,8},{1,5},{5,9},{2,6},{6,10},{3,7},{7,11},{16,20},{20,24},... | collective-permute-start | bytes 1474568 | tf_op jit(solution)/shard_map/ppermute | solution.py:116
  91.8 21.2 %collective-permute-start.28 = (bf16[320,768]{1,0:T(8,128)(2,1)}, bf16[320,768]{1,0:T(8,128)(2,1)}, u32[]{:S(2)}, u32[]{:S(2)}) collective-permute-start(bf16[320,768]{1,0:T(8,128)(2,1)} %get-tuple-element.43), channel_id=1, source_target_pairs={{8,4},{12,8},{9,5},{13,9},{10,6},{14,10},{11,7},{15,11},{24,20},{2... | collective-permute-start | bytes 1474568 | tf_op jit(solution)/shard_map/ppermute | solution.py:117
  97.7 2.2 %copy-start.8 = (bf16[256,640]{0,1:T(8,128)(2,1)S(1)}, bf16[256,640]{0,1:T(8,128)(2,1)}, u32[]{:S(2)}) copy-start(bf16[256,640]{0,1:T(8,128)(2,1)} %copy-done.7) | copy-start | bytes 983044
  97.7 2.2 %copy-start.11 = (bf16[256,640]{0,1:T(8,128)(2,1)S(1)}, bf16[256,640]{0,1:T(8,128)(2,1)}, u32[]{:S(2)}) copy-start(bf16[256,640]{0,1:T(8,128)(2,1)} %copy-done.10) | copy-start | bytes 983044
  104.8 32.0 %collective-permute-start.14 = (bf16[1024,640]{1,0:T(8,128)(2,1)}, bf16[1024,640]{1,0:T(8,128)(2,1)}, u32[]{:S(2)}, u32[]{:S(2)}) collective-permute-start(bf16[1024,640]{1,0:T(8,128)(2,1)} %convolution_convert_fusion.2), channel_id=1, source_target_pairs={{0,16},{16,0},{1,17},{17,1},{2,18},{18,2},{3,19},{19,3},{4,20},{20... | collective-permute-start | bytes 3932168 | tf_op jit(solution)/shard_map/ppermute | solution.py:137
  107.1 14.5 %collective-permute-start.20 = (bf16[320,512]{1,0:T(8,128)(2,1)}, bf16[320,512]{1,0:T(8,128)(2,1)}, u32[]{:S(2)}, u32[]{:S(2)}) collective-permute-start(bf16[320,512]{1,0:T(8,128)(2,1)} %get-tuple-element.34), channel_id=1, source_target_pairs={{0,4},{4,8},{8,12},{1,5},{5,9},{9,13},{2,6},{6,10},{10,14},{3,7},{... | collective-permute-start | bytes 983048 | tf_op jit(solution)/shard_map/ppermute | solution.py:116
  111.7 12.2 %collective-permute-start.23 = (bf16[320,512]{1,0:T(8,128)(2,1)}, bf16[320,512]{1,0:T(8,128)(2,1)}, u32[]{:S(2)}, u32[]{:S(2)}) collective-permute-start(bf16[320,512]{1,0:T(8,128)(2,1)} %get-tuple-element.35), channel_id=1, source_target_pairs={{4,0},{8,4},{12,8},{5,1},{9,5},{13,9},{6,2},{10,6},{14,10},{7,3},{... | collective-permute-start | bytes 983048 | tf_op jit(solution)/shard_map/ppermute | solution.py:117
  115.5 15.6 %collective-permute-start.26 = (bf16[320,768]{1,0:T(8,128)(2,1)}, bf16[320,768]{1,0:T(8,128)(2,1)S(1)}, u32[]{:S(2)}, u32[]{:S(2)}) collective-permute-start(bf16[320,768]{1,0:T(8,128)(2,1)} %get-tuple-element.40), channel_id=1, source_target_pairs={{0,4},{4,8},{8,12},{1,5},{5,9},{9,13},{2,6},{6,10},{10,14},{3,7},{... | collective-permute-start | bytes 1474568 | tf_op jit(solution)/shard_map/ppermute | solution.py:116
  120.1 15.2 %collective-permute-start.29 = (bf16[320,768]{1,0:T(8,128)(2,1)}, bf16[320,768]{1,0:T(8,128)(2,1)}, u32[]{:S(2)}, u32[]{:S(2)}) collective-permute-start(bf16[320,768]{1,0:T(8,128)(2,1)} %get-tuple-element.41), channel_id=1, source_target_pairs={{4,0},{8,4},{12,8},{5,1},{9,5},{13,9},{6,2},{10,6},{14,10},{7,3},{... | collective-permute-start | bytes 1474568 | tf_op jit(solution)/shard_map/ppermute | solution.py:117
  121.6 15.3 %copy-start.9 = (bf16[256,640]{0,1:T(8,128)(2,1)S(1)}, bf16[256,640]{0,1:T(8,128)(2,1)}, u32[]{:S(2)}) copy-start(bf16[256,640]{0,1:T(8,128)(2,1)} %copy-done.7) | copy-start | bytes 983044
  121.6 15.3 %copy-start.12 = (bf16[256,640]{0,1:T(8,128)(2,1)S(1)}, bf16[256,640]{0,1:T(8,128)(2,1)}, u32[]{:S(2)}) copy-start(bf16[256,640]{0,1:T(8,128)(2,1)} %copy-done.10) | copy-start | bytes 983044
  131.1 0.8 copy-start.6
  141.0 2.5 %copy-start.2 = (bf16[320,512]{1,0:T(8,128)(2,1)S(1)}, bf16[320,512]{1,0:T(8,128)(2,1)}, u32[]{:S(2)}) copy-start(bf16[320,512]{1,0:T(8,128)(2,1)} %fusion.17) | copy-start | bytes 983044
  142.1 10.7 %collective-permute-start.15 = (bf16[256,2,320]{0,2,1:T(8,128)(2,1)}, bf16[256,2,320]{0,2,1:T(8,128)(2,1)}, u32[]{:S(2)}, u32[]{:S(2)}) collective-permute-start(bf16[256,2,320]{0,2,1:T(8,128)(2,1)} %bitcast.103), channel_id=1, source_target_pairs={{0,1},{1,0},{2,3},{3,2},{4,5},{5,4},{6,7},{7,6},{8,9},{9,8},{10,11... | collective-permute-start | bytes 983048 | tf_op jit(solution)/shard_map/ppermute | solution.py:12
  145.6 15.7 %collective-permute-start.16 = (bf16[256,2,320]{0,2,1:T(8,128)(2,1)}, bf16[256,2,320]{0,2,1:T(8,128)(2,1)}, u32[]{:S(2)}, u32[]{:S(2)}) collective-permute-start(bf16[256,2,320]{0,2,1:T(8,128)(2,1)} %bitcast.23), channel_id=1, source_target_pairs={{0,2},{1,3},{2,0},{3,1},{4,6},{5,7},{6,4},{7,5},{8,10},{9,11},{10,... | collective-permute-start | bytes 983048 | tf_op jit(solution)/shard_map/ppermute | solution.py:12
  147.1 15.2 %collective-permute-start.17 = (bf16[256,2,320]{0,2,1:T(8,128)(2,1)}, bf16[256,2,320]{0,2,1:T(8,128)(2,1)S(1)}, u32[]{:S(2)}, u32[]{:S(2)}) collective-permute-start(bf16[256,2,320]{0,2,1:T(8,128)(2,1)} %bitcast.26), channel_id=1, source_target_pairs={{0,3},{1,2},{2,1},{3,0},{4,7},{5,6},{6,5},{7,4},{8,11},{9,10},{10,... | collective-permute-start | bytes 983048 | tf_op jit(solution)/shard_map/ppermute | solution.py:12
